TPU v7x, 768 devices: a whole 4x8x12 slice. The times are simulated.
768 devices in a mesh: group: 192 (over y, z, core), peer: 4 (over x).
Axes of the slice: x: 4, y: 8, z: 12, core: 2. Of those that a mesh axis runs over, the one named last changes fastest.
Arguments:
- queries: bfloat16 [98304, 1024], P(('group', 'peer')), may hold values from -40 to 40
- keys_values: bfloat16 [98304, 256], P(('group', 'peer')), may hold values from -40 to 40
- doc_lengths: int32 [25], replicated, may hold values from 1 to 4096, 98304 in all
Outputs:
- attended: bfloat16 [98304, 1024], P(('group', 'peer'))
- log_total: float32 [98304, 8], P(('group', 'peer'))
Inputs may be any that keep to these rules, and one draw needn't show every extreme that they name: `doc_lengths`: every document has 1 to 4096 tokens, the lengths sum to 98304, and one document has exactly 4096.
All inputs are finite; a program needn't handle non-finite values.
Results may differ from a plain program's by a relative error of at most 0.005.
Values may be sent and summed in bfloat16 or wider, within the bound.
No kernel may reach another device: no remote copies, remote signals or barrier semaphores. Data moves between devices by JAX's collectives and lax.ppermute only.
A program may use at most 32 MiB of HBM per device.

v0:
```python
import functools
import math

import jax
import jax.numpy as jnp
from jax import lax
from jax.experimental import pallas as pl
from jax.experimental.pallas import tpu as pltpu
from jax.sharding import PartitionSpec as P


ROWS = 128
HEADS = 8
WIDTH = 128
BLOCKS = 4
NEG = -1e30
LIMIT = 2.0**40
SCALE = math.log2(math.e) / math.sqrt(WIDTH)
F32 = jnp.float32
BF16 = jnp.bfloat16


def starts_at(doc_ref, pos):
    def step(d, carry):
        end, start = carry
        end = end + doc_ref[d]
        return end, jnp.where(end <= pos, end, start)

    return lax.fori_loop(0, doc_ref.shape[0], step, (jnp.int32(0), jnp.zeros_like(pos)), unroll=True)[1]


def prepare_body(own, doc_ref, q_ref, query, row_start):
    for h in range(HEADS):
        rows = slice(h // 2 * WIDTH, (h // 2 + 1) * WIDTH)
        query[rows, h % 2 * ROWS : (h % 2 + 1) * ROWS] = q_ref[:, h * WIDTH : (h + 1) * WIDTH].T
    group, peer = own()
    row_pos = (group * 4 + peer) * ROWS + lax.broadcasted_iota(jnp.int32, (8, ROWS), 1)
    row_start[...] = starts_at(doc_ref, row_pos)


def prepare(doc_lengths, queries, own):
    vmem = pl.BlockSpec(memory_space=pltpu.VMEM)
    return pl.pallas_call(
        functools.partial(prepare_body, own),
        out_shape=(pltpu.VMEM((HEADS // 2 * WIDTH, 2 * ROWS), BF16), pltpu.VMEM((8, ROWS), jnp.int32)),
        in_specs=[pl.BlockSpec(memory_space=pltpu.SMEM), vmem],
        out_specs=(vmem, vmem),
        compiler_params=pltpu.CompilerParams(vmem_limit_bytes=4 << 20),
    )(doc_lengths, queries)


def attend_body(first, last, places, own, doc_ref, query, start_ref, *refs):
    kv_refs, refs = refs[: len(places)], refs[len(places) :]
    if not first:
        stat_in, acc_in, refs = refs[0], refs[1], refs[2:]
    if last:
        out, log_out, stat, acc, bias = refs
    else:
        stat, acc, bias = refs
    group, peer = own()
    q_first = (group * 4 + peer) * ROWS

    start_low = starts_at(doc_ref, q_first)
    start_high = starts_at(doc_ref, q_first + ROWS - 1)
    row_pos = q_first + lax.broadcasted_iota(jnp.int32, (1, ROWS), 1)
    row_start = start_ref[:1]
    span = BLOCKS * ROWS

    def pair_rows(values, h):
        return jnp.concatenate([values[h : h + 1], values[h + 1 : h + 2]], axis=1)

    def operands(tile):
        values = jnp.concatenate([tile[:, WIDTH:].T, jnp.ones((16, span), BF16)], axis=0)
        return tile[:, :WIDTH], values

    def set_bias(base):
        key_pos = base + lax.broadcasted_iota(jnp.int32, (span, ROWS), 0)
        hidden = jnp.where((key_pos >= row_start) & (key_pos <= row_pos), F32(0), F32(NEG))
        bias[:, :ROWS] = hidden
        bias[:, ROWS:] = hidden

    def exact(tile, base):
        keys, values = operands(tile)
        set_bias(base)

        for p in range(HEADS // 2):
            h = 2 * p
            score = jnp.dot(keys, query[p * WIDTH : (p + 1) * WIDTH], preferred_element_type=F32) * F32(SCALE) + bias[...]
            old = pair_rows(stat, h)
            new = jnp.maximum(old, jnp.max(score, axis=0, keepdims=True))
            fade = jnp.exp2(old - new)
            part = jnp.dot(values, jnp.exp2(score - new).astype(BF16), preferred_element_type=F32)
            for k in range(2):
                rows, cols = slice((h + k) * WIDTH, (h + k + 1) * WIDTH), slice(k * ROWS, (k + 1) * ROWS)
                acc[rows] = acc[rows] * fade[:, cols] + part[:WIDTH, cols]
                at = HEADS + h + k
                stat[at : at + 1] = stat[at : at + 1] * fade[:, cols] + part[WIDTH : WIDTH + 1, cols]
                stat[h + k : h + k + 1] = new[:, cols]

    def quick(tile, base, masked):
        keys, values = operands(tile)
        if masked:
            set_bias(base)
        for p in range(HEADS // 2):
            h = 2 * p
            held = pair_rows(stat, h)
            score = jnp.dot(keys, query[p * WIDTH : (p + 1) * WIDTH], preferred_element_type=F32) * F32(SCALE) - held
            if masked:
                score = score + bias[...]
            part = jnp.dot(values, jnp.exp2(score).astype(BF16), preferred_element_type=F32)
            for k in range(2):
                rows, cols = slice((h + k) * WIDTH, (h + k + 1) * WIDTH), slice(k * ROWS, (k + 1) * ROWS)
                acc[rows] += part[:WIDTH, cols]
                at = HEADS + h + k
                stat[at : at + 1] += part[WIDTH : WIDTH + 1, cols]

    def run(fast):
        if first:
            stat[:HEADS] = jnp.full((HEADS, ROWS), NEG, F32)
            stat[HEADS:] = jnp.zeros((HEADS, ROWS), F32)
            acc[...] = jnp.zeros_like(acc)
        else:
            stat[...] = stat_in[...]
            acc[...] = acc_in[...]

        for n, (kv_ref, (slots, place)) in enumerate(zip(kv_refs, places)):

            def body(i, _, kv_ref=kv_ref, place=place, own_tile=first and n == 0):
                load, tile_group = place(kv_ref, i, group)
                base = tile_group * span
                needed = (base + span > start_low) & (base < q_first + ROWS) & (base >= 0)
                whole = (base >= start_high) & (base + span <= q_first)
                if not fast:

                    @pl.when(needed)
                    def _():
                        exact(load(), base)

                    return 0

                @pl.when(needed & whole)
                def _():
                    quick(load(), base, False)

                @pl.when(needed & jnp.logical_not(whole))
                def _():
                    quick(load(), base, True)

                return 0

            start = 0
            if fast and first and n == 0:
                load, tile_group = place(kv_ref, 0, group)
                exact(load(), tile_group * span)
                start = 1
            lax.fori_loop(start, slots, body, 0)

    run(True)

    @pl.when(jnp.logical_not(jnp.max(stat[HEADS:]) <= F32(LIMIT)))
    def _():
        run(False)

    if last:
        stats = stat[...]
        for h in range(HEADS):
            rows = slice(h * WIDTH, (h + 1) * WIDTH)
            out[:, rows] = (acc[rows] / stats[HEADS + h : HEADS + h + 1]).T.astype(BF16)
        log_out[...] = stats[:HEADS] * F32(math.log(2.0)) + jnp.log(stats[HEADS:])


def attend(doc_lengths, prepared, pieces, state, last, own):
    places = [(kv.shape[1] // ROWS, place) for kv, place in pieces]
    vmem = pl.BlockSpec(memory_space=pltpu.VMEM)
    arrays = (*prepared, *(kv for kv, _ in pieces), *(state or ()))
    operands = [doc_lengths, *(pltpu.with_memory_space_constraint(a, pltpu.VMEM) for a in arrays)]
    state_shape = [(2 * HEADS, ROWS), (HEADS * WIDTH, ROWS)]
    bias = pltpu.VMEM((BLOCKS * ROWS, 2 * ROWS), F32)
    if last:
        out_shape = (
            jax.ShapeDtypeStruct((ROWS, HEADS * WIDTH), BF16),
            jax.ShapeDtypeStruct((HEADS, ROWS), F32),
        )
        scratch = [pltpu.VMEM(s, F32) for s in state_shape] + [bias]
    else:
        out_shape = tuple(pltpu.VMEM(s, F32) for s in state_shape)
        scratch = [bias]
    return pl.pallas_call(
        functools.partial(attend_body, state is None, last, places, own),
        out_shape=out_shape,
        in_specs=[pl.BlockSpec(memory_space=pltpu.SMEM)] + [vmem] * (len(operands) - 1),
        out_specs=(vmem, vmem),
        scratch_shapes=scratch,
        compiler_params=pltpu.CompilerParams(vmem_limit_bytes=16 << 20),
    )(*operands)


AXES = ("group", "peer")


def tiles(of_other, groups):
    def at(kv_ref, i, group):
        def load():
            return kv_ref[:, pl.ds(pl.multiple_of(i * ROWS, ROWS), ROWS), :].reshape(BLOCKS * ROWS, 2 * WIDTH)

        line, core = group // 2, group % 2
        return load, groups(i, line, 1 - core if of_other else core)

    return at


def near(i, line, core):
    pair = 2 * (line - 1 - core) + jnp.where(i == 1, core, 1 - core)
    return jnp.where(i == 0, 2 * line + core, pair)


def far(i, line, core):
    return 2 * (line - 3 - core) + jnp.where(i == 0, core, 1 - core)


def own():
    return lax.axis_index("group"), lax.axis_index("peer")


def moved(value, source):
    count = lax.axis_size("group") * lax.axis_size("peer")
    pairs = [(source(t), t) for t in range(count) if source(t) >= 0]
    return lax.ppermute(value, AXES, pairs)


def gathered(value):
    return lax.all_to_all(jnp.broadcast_to(value, (BLOCKS, *value.shape)), "peer", 0, 0)


def shards(queries, keys_values, doc_lengths):
    chip = jnp.concatenate([keys_values, moved(keys_values, lambda t: t ^ 4)], axis=0)
    pair_near = moved(chip, lambda t: t - 8 - 8 * (t // 4 % 2))
    pair_far = moved(chip, lambda t: t - 24 - 8 * (t // 4 % 2))
    prepared = prepare(doc_lengths, queries, own)
    near_mine = gathered(jnp.concatenate([keys_values, pair_near], axis=0))
    far_mine = gathered(pair_far)
    near_other = moved(near_mine, lambda t: t ^ 4)
    far_other = moved(far_mine, lambda t: t ^ 4)
    state = attend(doc_lengths, prepared, [(near_mine, tiles(False, near))], None, False, own)
    state = attend(
        doc_lengths, prepared, [(near_other, tiles(True, near)), (far_mine, tiles(False, far))], state, False, own
    )
    attended, log_total = attend(doc_lengths, prepared, [(far_other, tiles(True, far))], state, True, own)
    return attended, log_total.T


def solution(mesh):
    placed = (P(AXES, None), P(AXES, None), P())
    return jax.shard_map(shards, mesh=mesh, in_specs=placed, out_specs=(P(AXES, None), P(AXES, None)), check_vma=False)
```

profile of v0, /device:TPU:49, one launch (start us, length us, event | category | flops | bytes accessed | tf_op | source)
XLA Modules:
  0.0 83.6 jit_solution(17666264738597552391)
XLA Ops:
  0.6 2.6 %collective-permute-start = (bf16[128,256]{1,0:T(8,128)(2,1)}, bf16[128,256]{1,0:T(8,128)(2,1)S(1)}, u32[]{:S(2)}, u32[]{:S(2)}) collective-permute-start(bf16[128,256]{1,0:T(8,128)(2,1)} %param.4), channel_id=1, source_target_pairs={{4,0},{5,1},{6,2},{7,3},{0,4},{1,5},{2,6},{3,7},{12,8},{13,9},{14,... | collective-permute-start | bytes 196616 | tf_op jit(solution)/shard_map/ppermute | solution.py:228
  3.2 0.8 %constant_dynamic-update-slice_fusion.1 = bf16[256,256]{1,0:T(8,128)(2,1)S(1)} fusion(bf16[128,256]{1,0:T(8,128)(2,1)} %param.4), kind=kLoop, calls=%fused_computation.2 | loop fusion | bytes 131072
  4.1 0.0 copy-start.2
  4.1 0.2 collective-permute-done
  4.3 5.8 %collective-permute-start.3 = (bf16[256,256]{1,0:T(8,128)(2,1)S(1)}, bf16[256,256]{1,0:T(8,128)(2,1)S(1)}, u32[]{:S(2)}, u32[]{:S(2)}) collective-permute-start(bf16[256,256]{1,0:T(8,128)(2,1)S(1)} %constant_dynamic-update-slice_fusion), channel_id=1, source_target_pairs={{0,8},{1,9},{2,10},{3,11},{8,16},{9,17},{10,18},{11,19},{4,20},{5,... | collective-permute-start | bytes 393224 | tf_op jit(solution)/shard_map/ppermute | solution.py:228
  10.1 11.7 %collective-permute-done.3 = bf16[256,256]{1,0:T(8,128)(2,1)S(1)} collective-permute-done((bf16[256,256]{1,0:T(8,128)(2,1)S(1)}, bf16[256,256]{1,0:T(8,128)(2,1)S(1)}, u32[]{:S(2)}, u32[]{:S(2)}) %collective-permute-start.3) | collective-permute-done | bytes 131104 | tf_op jit(solution)/shard_map/ppermute | solution.py:228
  21.8 0.0 copy-done.2
  21.9 1.0 %broadcast_in_dim.7 = bf16[4,384,256]{2,1,0:T(8,128)(2,1)} broadcast(bf16[384,256]{1,0:T(8,128)(2,1)S(1)} %pad_maximum_fusion), dimensions={1,2} | broadcast | bytes 983040 | tf_op jit(solution)/shard_map/broadcast_in_dim | solution.py:232
  22.8 4.0 %all-to-all-start.1 = ((bf16[4,384,256]{2,1,0:T(8,128)(2,1)}), bf16[4,384,256]{2,1,0:T(8,128)(2,1)S(1)}, u32[]{:S(2)}, u32[]{:S(2)}) async-start(bf16[4,384,256]{2,1,0:T(8,128)(2,1)} %broadcast_in_dim.7), calls=%async_computation.1 | async-start | bytes 1572864 | tf_op jit(solution)/shard_map/all_to_all | solution.py:232
  26.8 1.9 %collective-permute-start.1 = (bf16[256,256]{1,0:T(8,128)(2,1)S(1)}, bf16[256,256]{1,0:T(8,128)(2,1)S(1)}, u32[]{:S(2)}, u32[]{:S(2)}) collective-permute-start(bf16[256,256]{1,0:T(8,128)(2,1)S(1)} %constant_dynamic-update-slice_fusion), channel_id=1, source_target_pairs={{0,24},{1,25},{2,26},{3,27},{8,32},{9,33},{10,34},{11,35},{4,36},{... | collective-permute-start | bytes 393224 | tf_op jit(solution)/shard_map/ppermute | solution.py:228
  28.7 9.3 %collective-permute-done.1 = bf16[256,256]{1,0:T(8,128)(2,1)S(1)} collective-permute-done((bf16[256,256]{1,0:T(8,128)(2,1)S(1)}, bf16[256,256]{1,0:T(8,128)(2,1)S(1)}, u32[]{:S(2)}, u32[]{:S(2)}) %collective-permute-start.1) | collective-permute-done | bytes 131104 | tf_op jit(solution)/shard_map/ppermute | solution.py:228
  38.0 0.0 all-to-all-done.1.refs_0_
  38.0 0.8 broadcast_in_dim.6
  38.9 0.0 copy-start
  38.9 0.0 copy-start.1
  38.9 4.1 %all-to-all-start = ((bf16[4,256,256]{2,1,0:T(8,128)(2,1)}), bf16[4,256,256]{2,1,0:T(8,128)(2,1)S(1)}, u32[]{:S(2)}, u32[]{:S(2)}) async-start(bf16[4,256,256]{2,1,0:T(8,128)(2,1)} %broadcast_in_dim.6), calls=%async_computation | async-start | bytes 1048576 | tf_op jit(solution)/shard_map/all_to_all | solution.py:232
  42.9 9.1 %collective-permute-start.4 = (bf16[4,384,256]{2,1,0:T(8,128)(2,1)S(1)}, bf16[4,384,256]{2,1,0:T(8,128)(2,1)S(1)}, u32[]{:S(2)}, u32[]{:S(2)}) collective-permute-start(bf16[4,384,256]{2,1,0:T(8,128)(2,1)S(1)} %all-to-all-done.1.refs_0_), channel_id=1, source_target_pairs={{4,0},{5,1},{6,2},{7,3},{0,4},{1,5},{2,6},{3,7},{12,8},{13,9},{14,... | collective-permute-start | bytes 2359304 | tf_op jit(solution)/shard_map/ppermute | solution.py:228
  52.0 0.0 all-to-all-done.refs_1_
  52.0 8.1 %collective-permute-start.2 = (bf16[4,256,256]{2,1,0:T(8,128)(2,1)S(1)}, bf16[4,256,256]{2,1,0:T(8,128)(2,1)S(1)}, u32[]{:S(2)}, u32[]{:S(2)}) collective-permute-start(bf16[4,256,256]{2,1,0:T(8,128)(2,1)S(1)} %all-to-all-done.refs_1_), channel_id=1, source_target_pairs={{4,0},{5,1},{6,2},{7,3},{0,4},{1,5},{2,6},{3,7},{12,8},{13,9},{14,... | collective-permute-start | bytes 1572872 | tf_op jit(solution)/shard_map/ppermute | solution.py:228
  60.1 0.0 copy-done
  60.1 0.0 copy-done.1
  60.1 0.7 shard_map.50
  60.8 5.1 %shard_map.51 = (f32[16,128]{1,0:T(8,128)S(1)}, f32[1024,128]{1,0:T(8,128)S(1)}) custom-call(s32[25]{0:T(128)S(1)} %copy-done.1, bf16[512,256]{1,0:T(8,128)(2,1)S(1)} %get-tuple-element.10.query, s32[8,128]{1,0:T(8,128)S(1)} %get-tuple-element.11.start_ref, bf16[4,384,256]{2,1,0:T(8,128)(2,1)S(1)} %all-to-all-done.1.refs_0_), custom_call_target="tpu_custom_call" | custom-call | tf_op jit(solution)/shard_map/pallas_call | solution.py:188
  65.9 0.0 collective-permute-done.4.refs_0_
  65.9 13.4 %shard_map.52 = (f32[16,128]{1,0:T(8,128)S(1)}, f32[1024,128]{1,0:T(8,128)S(1)}) custom-call(s32[25]{0:T(128)S(1)} %copy-done.1, bf16[512,256]{1,0:T(8,128)(2,1)S(1)} %get-tuple-element.10.query, s32[8,128]{1,0:T(8,128)S(1)} %get-tuple-element.11.start_ref, bf16[4,384,256]{2,1,0:T(8,128)(2,1)S(1)} %collective-permute-done.4.refs_0_, ...), custom_call_target="tpu_custom_call" | custom-call | tf_op jit(solution)/shard_map/pallas_call | solution.py:188
  79.3 0.0 collective-permute-done.2.refs_0_
  79.3 4.3 %shard_map.53 = (bf16[128,1024]{1,0:T(8,128)(2,1)}, f32[8,128]{1,0:T(8,128)}) custom-call(s32[25]{0:T(128)S(1)} %copy-done.1, bf16[512,256]{1,0:T(8,128)(2,1)S(1)} %get-tuple-element.10.query, s32[8,128]{1,0:T(8,128)S(1)} %get-tuple-element.11.start_ref, bf16[4,256,256]{2,1,0:T(8,128)(2,1)S(1)} %collective-permute-done.2.refs_0_, ...), custom_call_target="tpu_custom_call" | custom-call | tf_op jit(solution)/shard_map/pallas_call | solution.py:188
  (2 shorter events, 0.0 us)
Async XLA Ops:
  0.6 3.7 %collective-permute-start = (bf16[128,256]{1,0:T(8,128)(2,1)}, bf16[128,256]{1,0:T(8,128)(2,1)S(1)}, u32[]{:S(2)}, u32[]{:S(2)}) collective-permute-start(bf16[128,256]{1,0:T(8,128)(2,1)} %param.4), channel_id=1, source_target_pairs={{4,0},{5,1},{6,2},{7,3},{0,4},{1,5},{2,6},{3,7},{12,8},{13,9},{14,... | collective-permute-start | bytes 196616 | tf_op jit(solution)/shard_map/ppermute | solution.py:228
  4.1 17.8 %copy-start.2 = (bf16[128,256]{1,0:T(8,128)(2,1)S(1)}, bf16[128,256]{1,0:T(8,128)(2,1)}, u32[]{:S(2)}) copy-start(bf16[128,256]{1,0:T(8,128)(2,1)} %param.4) | copy-start | bytes 196612
  4.3 17.5 %collective-permute-start.3 = (bf16[256,256]{1,0:T(8,128)(2,1)S(1)}, bf16[256,256]{1,0:T(8,128)(2,1)S(1)}, u32[]{:S(2)}, u32[]{:S(2)}) collective-permute-start(bf16[256,256]{1,0:T(8,128)(2,1)S(1)} %constant_dynamic-update-slice_fusion), channel_id=1, source_target_pairs={{0,8},{1,9},{2,10},{3,11},{8,16},{9,17},{10,18},{11,19},{4,20},{5,... | collective-permute-start | bytes 393224 | tf_op jit(solution)/shard_map/ppermute | solution.py:228
  22.8 15.2 %all-to-all-start.1 = ((bf16[4,384,256]{2,1,0:T(8,128)(2,1)}), bf16[4,384,256]{2,1,0:T(8,128)(2,1)S(1)}, u32[]{:S(2)}, u32[]{:S(2)}) async-start(bf16[4,384,256]{2,1,0:T(8,128)(2,1)} %broadcast_in_dim.7), calls=%async_computation.1 | async-start | bytes 1572864 | tf_op jit(solution)/shard_map/all_to_all | solution.py:232
  26.8 11.2 %collective-permute-start.1 = (bf16[256,256]{1,0:T(8,128)(2,1)S(1)}, bf16[256,256]{1,0:T(8,128)(2,1)S(1)}, u32[]{:S(2)}, u32[]{:S(2)}) collective-permute-start(bf16[256,256]{1,0:T(8,128)(2,1)S(1)} %constant_dynamic-update-slice_fusion), channel_id=1, source_target_pairs={{0,24},{1,25},{2,26},{3,27},{8,32},{9,33},{10,34},{11,35},{4,36},{... | collective-permute-start | bytes 393224 | tf_op jit(solution)/shard_map/ppermute | solution.py:228
  38.9 21.3 %copy-start = (bf16[128,1024]{1,0:T(8,128)(2,1)S(1)}, bf16[128,1024]{1,0:T(8,128)(2,1)}, u32[]{:S(2)}) copy-start(bf16[128,1024]{1,0:T(8,128)(2,1)} %q_ref.1) | copy-start | bytes 786436
  38.9 21.3 %copy-start.1 = (s32[25]{0:T(128)S(1)}, s32[25]{0:T(128)}, u32[]{:S(2)}) copy-start(s32[25]{0:T(128)} %doc_ref.7) | copy-start | bytes 304
  38.9 13.2 %all-to-all-start = ((bf16[4,256,256]{2,1,0:T(8,128)(2,1)}), bf16[4,256,256]{2,1,0:T(8,128)(2,1)S(1)}, u32[]{:S(2)}, u32[]{:S(2)}) async-start(bf16[4,256,256]{2,1,0:T(8,128)(2,1)} %broadcast_in_dim.6), calls=%async_computation | async-start | bytes 1048576 | tf_op jit(solution)/shard_map/all_to_all | solution.py:232
  42.9 23.0 %collective-permute-start.4 = (bf16[4,384,256]{2,1,0:T(8,128)(2,1)S(1)}, bf16[4,384,256]{2,1,0:T(8,128)(2,1)S(1)}, u32[]{:S(2)}, u32[]{:S(2)}) collective-permute-start(bf16[4,384,256]{2,1,0:T(8,128)(2,1)S(1)} %all-to-all-done.1.refs_0_), channel_id=1, source_target_pairs={{4,0},{5,1},{6,2},{7,3},{0,4},{1,5},{2,6},{3,7},{12,8},{13,9},{14,... | collective-permute-start | bytes 2359304 | tf_op jit(solution)/shard_map/ppermute | solution.py:228
  52.0 27.3 %collective-permute-start.2 = (bf16[4,256,256]{2,1,0:T(8,128)(2,1)S(1)}, bf16[4,256,256]{2,1,0:T(8,128)(2,1)S(1)}, u32[]{:S(2)}, u32[]{:S(2)}) collective-permute-start(bf16[4,256,256]{2,1,0:T(8,128)(2,1)S(1)} %all-to-all-done.refs_1_), channel_id=1, source_target_pairs={{4,0},{5,1},{6,2},{7,3},{0,4},{1,5},{2,6},{3,7},{12,8},{13,9},{14,... | collective-permute-start | bytes 1572872 | tf_op jit(solution)/shard_map/ppermute | solution.py:228
where the time goes:
time: 84 us; the launch traced here: 83.6 us
  starting transfers between devices  35.5 us (42%)
  Pallas kernels  23.4 us (28%)
  waiting for transfers between devices  21.2 us (25%)
  local copies, waits for them, and re-layouts  2.65 us (3%)
    ppermute x5, starting transfers between devices, moved(): return lax.ppermute(value, AXES, pairs)  27.4 us
    pallas_call x3, Pallas kernels, attend(): pl.pallas_call(functools.partial(attend_body, state is None, last, places...  22.8 us
    ppermute x5, waiting for transfers between devices, moved(): return lax.ppermute(value, AXES, pairs)  21.2 us
    all_to_all x2, starting transfers between devices, gathered(): lax.all_to_all(jnp.broadcast_to(value, (BLOCKS, *value.shape)), 'peer', 0...  8.1 us
    broadcast_in_dim x2, local copies, waits for them, and re-layouts, gathered(): jnp.broadcast_to(value, (BLOCKS, *value.shape))  1.78 us
  transfers between devices with their start and end apart: 7, of which 3 were waited for; matrix products, arithmetic and copies ran while one was open for 1% of the time, Pallas kernels for 23%

commit v1 on v0

--- a/solution.py
+++ b/solution.py
@@ -73,15 +73,18 @@
         values = jnp.concatenate([tile[:, WIDTH:].T, jnp.ones((16, span), BF16)], axis=0)
         return tile[:, :WIDTH], values
 
-    def set_bias(base):
-        key_pos = base + lax.broadcasted_iota(jnp.int32, (span, ROWS), 0)
-        hidden = jnp.where((key_pos >= row_start) & (key_pos <= row_pos), F32(0), F32(NEG))
-        bias[:, :ROWS] = hidden
-        bias[:, ROWS:] = hidden
-
-    def exact(tile, base):
+    def set_bias(base, order):
+        for n, place in enumerate(order):
+            if not isinstance(order, range):
+                place = (peer + place) % BLOCKS
+            key_pos = base + place * ROWS + lax.broadcasted_iota(jnp.int32, (ROWS, ROWS), 0)
+            hidden = jnp.where((key_pos >= row_start) & (key_pos <= row_pos), F32(0), F32(NEG))
+            bias[n * ROWS : (n + 1) * ROWS, :ROWS] = hidden
+            bias[n * ROWS : (n + 1) * ROWS, ROWS:] = hidden
+
+    def exact(tile, base, order):
         keys, values = operands(tile)
-        set_bias(base)
+        set_bias(base, order)
 
         for p in range(HEADS // 2):
             h = 2 * p
@@ -97,10 +100,10 @@
                 stat[at : at + 1] = stat[at : at + 1] * fade[:, cols] + part[WIDTH : WIDTH + 1, cols]
                 stat[h + k : h + k + 1] = new[:, cols]
 
-    def quick(tile, base, masked):
+    def quick(tile, base, order, masked):
         keys, values = operands(tile)
         if masked:
-            set_bias(base)
+            set_bias(base, order)
         for p in range(HEADS // 2):
             h = 2 * p
             held = pair_rows(stat, h)
@@ -126,7 +129,7 @@
         for n, (kv_ref, (slots, place)) in enumerate(zip(kv_refs, places)):
 
             def body(i, _, kv_ref=kv_ref, place=place, own_tile=first and n == 0):
-                load, tile_group = place(kv_ref, i, group)
+                load, tile_group, order = place(kv_ref, i, group)
                 base = tile_group * span
                 needed = (base + span > start_low) & (base < q_first + ROWS) & (base >= 0)
                 whole = (base >= start_high) & (base + span <= q_first)
@@ -134,24 +137,24 @@
 
                     @pl.when(needed)
                     def _():
-                        exact(load(), base)
+                        exact(load(), base, order)
 
                     return 0
 
                 @pl.when(needed & whole)
                 def _():
-                    quick(load(), base, False)
+                    quick(load(), base, order, False)
 
                 @pl.when(needed & jnp.logical_not(whole))
                 def _():
-                    quick(load(), base, True)
+                    quick(load(), base, order, True)
 
                 return 0
 
             start = 0
             if fast and first and n == 0:
-                load, tile_group = place(kv_ref, 0, group)
-                exact(load(), tile_group * span)
+                load, tile_group, order = place(kv_ref, 0, group)
+                exact(load(), tile_group * span, order)
                 start = 1
             lax.fori_loop(start, slots, body, 0)
 
@@ -196,15 +199,16 @@
 
 
 AXES = ("group", "peer")
-
-
-def tiles(of_other, groups):
+TURNS = (0, 1, 3, 2)
+
+
+def tiles(of_other, groups, turned=False):
     def at(kv_ref, i, group):
         def load():
             return kv_ref[:, pl.ds(pl.multiple_of(i * ROWS, ROWS), ROWS), :].reshape(BLOCKS * ROWS, 2 * WIDTH)
 
         line, core = group // 2, group % 2
-        return load, groups(i, line, 1 - core if of_other else core)
+        return load, groups(i, line, 1 - core if of_other else core), TURNS if turned else range(BLOCKS)
 
     return at
 
@@ -238,14 +242,17 @@
     pair_far = moved(chip, lambda t: t - 24 - 8 * (t // 4 % 2))
     prepared = prepare(doc_lengths, queries, own)
     near_mine = gathered(jnp.concatenate([keys_values, pair_near], axis=0))
-    far_mine = gathered(pair_far)
+    turns = []
+    for k in (1, 3, 2):
+        turns.append(moved(pair_far, lambda t, k=k: t // 4 * 4 + (t + k) % 4))
+    far_mine = jnp.concatenate([pair_far, *turns], axis=0).reshape(BLOCKS, *pair_far.shape)
     near_other = moved(near_mine, lambda t: t ^ 4)
     far_other = moved(far_mine, lambda t: t ^ 4)
     state = attend(doc_lengths, prepared, [(near_mine, tiles(False, near))], None, False, own)
     state = attend(
-        doc_lengths, prepared, [(near_other, tiles(True, near)), (far_mine, tiles(False, far))], state, False, own
+        doc_lengths, prepared, [(near_other, tiles(True, near)), (far_mine, tiles(False, far, True))], state, False, own
     )
-    attended, log_total = attend(doc_lengths, prepared, [(far_other, tiles(True, far))], state, True, own)
+    attended, log_total = attend(doc_lengths, prepared, [(far_other, tiles(True, far, True))], state, True, own)
     return attended, log_total.T
 
 

time: 84 us -> 85.8 us (1.021)
  waiting for transfers between devices: 21.2 us -> 23 us
    all_to_all x2 -> x1, waiting for transfers between devices: 0.01 us -> 6.36 us  [gathered(): lax.all_to_all(jnp.broadcast_to(value, (BLOCKS, *value.shape)), 'peer', 0...]
    ppermute x5 -> x8, starting transfers between devices: 27.4 us -> 32.3 us  [moved(): return lax.ppermute(value, AXES, pairs)]
    ppermute x5 -> x8, waiting for transfers between devices: 21.2 us -> 16.6 us  [moved(): return lax.ppermute(value, AXES, pairs)]
    all_to_all x2 -> x1, starting transfers between devices: 8.1 us -> 4.01 us  [gathered(): lax.all_to_all(jnp.broadcast_to(value, (BLOCKS, *value.shape)), 'peer', 0...]
    broadcast_in_dim x2 -> x1, local copies, waits for them, and re-layouts: 1.78 us -> 0.95 us  [gathered(): jnp.broadcast_to(value, (BLOCKS, *value.shape))]
  transfers between devices with their start and end apart: 7 -> 9, of which waited for: 3 -> 5; matrix products, arithmetic and copies ran while one was open for 1% -> 1% of each run, Pallas kernels for 23% -> 22%
where the time goes in v1:
time: 85.8 us; the launch traced here: 85.4 us
  starting transfers between devices  36.3 us (42%)
  Pallas kernels  23.4 us (27%)
  waiting for transfers between devices  23 us (27%)
  local copies, waits for them, and re-layouts  1.82 us (2%)
    ppermute x8, starting transfers between devices, moved(): return lax.ppermute(value, AXES, pairs)  32.3 us
    pallas_call x3, Pallas kernels, attend(): pl.pallas_call(functools.partial(attend_body, state is None, last, places...  22.8 us
    ppermute x8, waiting for transfers between devices, moved(): return lax.ppermute(value, AXES, pairs)  16.6 us
    all_to_all x1, waiting for transfers between devices, gathered(): lax.all_to_all(jnp.broadcast_to(value, (BLOCKS, *value.shape)), 'peer', 0...  6.36 us
    all_to_all x1, starting transfers between devices, gathered(): lax.all_to_all(jnp.broadcast_to(value, (BLOCKS, *value.shape)), 'peer', 0...  4.01 us
  transfers between devices with their start and end apart: 9, of which 5 were waited for; matrix products, arithmetic and copies ran while one was open for 1% of the time, Pallas kernels for 22%

profile of v1, /device:TPU:49, one launch (start us, length us, event | category | flops | bytes accessed | tf_op | source)
XLA Modules:
  0.0 85.4 jit_solution(10277452883714437761)
XLA Ops:
  0.6 2.6 %collective-permute-start = (bf16[128,256]{1,0:T(8,128)(2,1)}, bf16[128,256]{1,0:T(8,128)(2,1)S(1)}, u32[]{:S(2)}, u32[]{:S(2)}) collective-permute-start(bf16[128,256]{1,0:T(8,128)(2,1)} %param.4), channel_id=1, source_target_pairs={{4,0},{5,1},{6,2},{7,3},{0,4},{1,5},{2,6},{3,7},{12,8},{13,9},{14,... | collective-permute-start | bytes 196616 | tf_op jit(solution)/shard_map/ppermute | solution.py:232
  3.2 0.8 constant_dynamic-update-slice_fusion.1
  4.1 0.0 copy-start.2
  4.1 0.2 collective-permute-done
  4.3 5.8 %collective-permute-start.6 = (bf16[256,256]{1,0:T(8,128)(2,1)S(1)}, bf16[256,256]{1,0:T(8,128)(2,1)S(1)}, u32[]{:S(2)}, u32[]{:S(2)}) collective-permute-start(bf16[256,256]{1,0:T(8,128)(2,1)S(1)} %constant_dynamic-update-slice_fusion), channel_id=1, source_target_pairs={{0,8},{1,9},{2,10},{3,11},{8,16},{9,17},{10,18},{11,19},{4,20},{5,... | collective-permute-start | bytes 393224 | tf_op jit(solution)/shard_map/ppermute | solution.py:232
  10.1 11.7 %collective-permute-done.6 = bf16[256,256]{1,0:T(8,128)(2,1)S(1)} collective-permute-done((bf16[256,256]{1,0:T(8,128)(2,1)S(1)}, bf16[256,256]{1,0:T(8,128)(2,1)S(1)}, u32[]{:S(2)}, u32[]{:S(2)}) %collective-permute-start.6) | collective-permute-done | bytes 131104 | tf_op jit(solution)/shard_map/ppermute | solution.py:232
  21.8 0.0 copy-done.2
  21.9 1.0 %broadcast_in_dim.3 = bf16[4,384,256]{2,1,0:T(8,128)(2,1)} broadcast(bf16[384,256]{1,0:T(8,128)(2,1)S(1)} %pad_maximum_fusion.1), dimensions={1,2} | broadcast | bytes 983040 | tf_op jit(solution)/shard_map/broadcast_in_dim | solution.py:236
  22.8 4.0 %all-to-all-start = ((bf16[4,384,256]{2,1,0:T(8,128)(2,1)}), bf16[4,384,256]{2,1,0:T(8,128)(2,1)S(1)}, u32[]{:S(2)}, u32[]{:S(2)}) async-start(bf16[4,384,256]{2,1,0:T(8,128)(2,1)} %broadcast_in_dim.3), calls=%async_computation | async-start | bytes 1572864 | tf_op jit(solution)/shard_map/all_to_all | solution.py:236
  26.8 0.0 copy-start
  26.8 2.0 %collective-permute-start.1 = (bf16[256,256]{1,0:T(8,128)(2,1)S(1)}, bf16[256,256]{1,0:T(8,128)(2,1)S(1)}, u32[]{:S(2)}, u32[]{:S(2)}) collective-permute-start(bf16[256,256]{1,0:T(8,128)(2,1)S(1)} %constant_dynamic-update-slice_fusion), channel_id=1, source_target_pairs={{0,24},{1,25},{2,26},{3,27},{8,32},{9,33},{10,34},{11,35},{4,36},{... | collective-permute-start | bytes 393224 | tf_op jit(solution)/shard_map/ppermute | solution.py:232
  28.9 6.4 %all-to-all-done.refs_0_ = bf16[4,384,256]{2,1,0:T(8,128)(2,1)S(1)} async-done(((bf16[4,384,256]{2,1,0:T(8,128)(2,1)}), bf16[4,384,256]{2,1,0:T(8,128)(2,1)S(1)}, u32[]{:S(2)}, u32[]{:S(2)}) %all-to-all-start) | async-done | bytes 786464 | tf_op jit(solution)/shard_map/all_to_all | solution.py:236
  35.2 6.7 %collective-permute-start.7 = (bf16[4,384,256]{2,1,0:T(8,128)(2,1)S(1)}, bf16[4,384,256]{2,1,0:T(8,128)(2,1)S(1)}, u32[]{:S(2)}, u32[]{:S(2)}) collective-permute-start(bf16[4,384,256]{2,1,0:T(8,128)(2,1)S(1)} %all-to-all-done.refs_0_), channel_id=1, source_target_pairs={{4,0},{5,1},{6,2},{7,3},{0,4},{1,5},{2,6},{3,7},{12,8},{13,9},{14,... | collective-permute-start | bytes 2359304 | tf_op jit(solution)/shard_map/ppermute | solution.py:232
  42.0 0.0 collective-permute-done.1
  42.0 2.8 %collective-permute-start.2 = (bf16[256,256]{1,0:T(8,128)(2,1)S(1)}, bf16[256,256]{1,0:T(8,128)(2,1)S(1)}, u32[]{:S(2)}, u32[]{:S(2)}) collective-permute-start(bf16[256,256]{1,0:T(8,128)(2,1)S(1)} %collective-permute-done.1), channel_id=1, source_target_pairs={{1,0},{2,1},{3,2},{0,3},{5,4},{6,5},{7,6},{4,7},{9,8},{10,9},{11,1... | collective-permute-start | bytes 393224 | tf_op jit(solution)/shard_map/ppermute | solution.py:232
  44.8 2.5 %collective-permute-start.3 = (bf16[256,256]{1,0:T(8,128)(2,1)S(1)}, bf16[256,256]{1,0:T(8,128)(2,1)S(1)}, u32[]{:S(2)}, u32[]{:S(2)}) collective-permute-start(bf16[256,256]{1,0:T(8,128)(2,1)S(1)} %collective-permute-done.1), channel_id=1, source_target_pairs={{3,0},{0,1},{1,2},{2,3},{7,4},{4,5},{5,6},{6,7},{11,8},{8,9},{9,10... | collective-permute-start | bytes 393224 | tf_op jit(solution)/shard_map/ppermute | solution.py:232
  47.3 2.5 %collective-permute-start.4 = (bf16[256,256]{1,0:T(8,128)(2,1)S(1)}, bf16[256,256]{1,0:T(8,128)(2,1)S(1)}, u32[]{:S(2)}, u32[]{:S(2)}) collective-permute-start(bf16[256,256]{1,0:T(8,128)(2,1)S(1)} %collective-permute-done.1), channel_id=1, source_target_pairs={{2,0},{3,1},{0,2},{1,3},{6,4},{7,5},{4,6},{5,7},{10,8},{11,9},{8,1... | collective-permute-start | bytes 393224 | tf_op jit(solution)/shard_map/ppermute | solution.py:232
  49.8 0.0 collective-permute-done.2
  49.8 1.9 %collective-permute-done.3 = bf16[256,256]{1,0:T(8,128)(2,1)S(1)} collective-permute-done((bf16[256,256]{1,0:T(8,128)(2,1)S(1)}, bf16[256,256]{1,0:T(8,128)(2,1)S(1)}, u32[]{:S(2)}, u32[]{:S(2)}) %collective-permute-start.3) | collective-permute-done | bytes 131104 | tf_op jit(solution)/shard_map/ppermute | solution.py:232
  51.7 2.8 %collective-permute-done.4 = bf16[256,256]{1,0:T(8,128)(2,1)S(1)} collective-permute-done((bf16[256,256]{1,0:T(8,128)(2,1)S(1)}, bf16[256,256]{1,0:T(8,128)(2,1)S(1)}, u32[]{:S(2)}, u32[]{:S(2)}) %collective-permute-start.4) | collective-permute-done | bytes 131104 | tf_op jit(solution)/shard_map/ppermute | solution.py:232
  54.5 0.0 copy-start.1
  54.5 7.3 %collective-permute-start.5 = (bf16[4,256,256]{2,1,0:T(8,128)(2,1)S(1)}, bf16[4,256,256]{2,1,0:T(8,128)(2,1)S(1)}, u32[]{:S(2)}, u32[]{:S(2)}) collective-permute-start(bf16[4,256,256]{2,1,0:T(8,128)(2,1)S(1)} %bitcast.2), channel_id=1, source_target_pairs={{4,0},{5,1},{6,2},{7,3},{0,4},{1,5},{2,6},{3,7},{12,8},{13,9},{14,... | collective-permute-start | bytes 1572872 | tf_op jit(solution)/shard_map/ppermute | solution.py:232
  61.9 0.0 copy-done
  61.9 0.0 copy-done.1
  61.9 0.7 shard_map.50
  62.6 5.1 %shard_map.51 = (f32[16,128]{1,0:T(8,128)S(1)}, f32[1024,128]{1,0:T(8,128)S(1)}) custom-call(s32[25]{0:T(128)S(1)} %copy-done.1, bf16[512,256]{1,0:T(8,128)(2,1)S(1)} %get-tuple-element.10.query, s32[8,128]{1,0:T(8,128)S(1)} %get-tuple-element.11.start_ref, bf16[4,384,256]{2,1,0:T(8,128)(2,1)S(1)} %all-to-all-done.refs_0_), custom_call_target="tpu_custom_call" | custom-call | tf_op jit(solution)/shard_map/pallas_call | solution.py:191
  67.7 0.0 collective-permute-done.7.refs_0_
  67.7 13.4 %shard_map.52 = (f32[16,128]{1,0:T(8,128)S(1)}, f32[1024,128]{1,0:T(8,128)S(1)}) custom-call(s32[25]{0:T(128)S(1)} %copy-done.1, bf16[512,256]{1,0:T(8,128)(2,1)S(1)} %get-tuple-element.10.query, s32[8,128]{1,0:T(8,128)S(1)} %get-tuple-element.11.start_ref, bf16[4,384,256]{2,1,0:T(8,128)(2,1)S(1)} %collective-permute-done.7.refs_0_, ...), custom_call_target="tpu_custom_call" | custom-call | tf_op jit(solution)/shard_map/pallas_call | solution.py:191
  81.1 0.0 collective-permute-done.5.refs_0_
  81.1 4.3 %shard_map.53 = (bf16[128,1024]{1,0:T(8,128)(2,1)}, f32[8,128]{1,0:T(8,128)}) custom-call(s32[25]{0:T(128)S(1)} %copy-done.1, bf16[512,256]{1,0:T(8,128)(2,1)S(1)} %get-tuple-element.10.query, s32[8,128]{1,0:T(8,128)S(1)} %get-tuple-element.11.start_ref, bf16[4,256,256]{2,1,0:T(8,128)(2,1)S(1)} %collective-permute-done.5.refs_0_, ...), custom_call_target="tpu_custom_call" | custom-call | tf_op jit(solution)/shard_map/pallas_call | solution.py:191
  (3 shorter events, 0.1 us)
Async XLA Ops:
  0.6 3.7 %collective-permute-start = (bf16[128,256]{1,0:T(8,128)(2,1)}, bf16[128,256]{1,0:T(8,128)(2,1)S(1)}, u32[]{:S(2)}, u32[]{:S(2)}) collective-permute-start(bf16[128,256]{1,0:T(8,128)(2,1)} %param.4), channel_id=1, source_target_pairs={{4,0},{5,1},{6,2},{7,3},{0,4},{1,5},{2,6},{3,7},{12,8},{13,9},{14,... | collective-permute-start | bytes 196616 | tf_op jit(solution)/shard_map/ppermute | solution.py:232
  4.1 17.8 %copy-start.2 = (bf16[128,256]{1,0:T(8,128)(2,1)S(1)}, bf16[128,256]{1,0:T(8,128)(2,1)}, u32[]{:S(2)}) copy-start(bf16[128,256]{1,0:T(8,128)(2,1)} %param.4) | copy-start | bytes 196612
  4.3 17.5 %collective-permute-start.6 = (bf16[256,256]{1,0:T(8,128)(2,1)S(1)}, bf16[256,256]{1,0:T(8,128)(2,1)S(1)}, u32[]{:S(2)}, u32[]{:S(2)}) collective-permute-start(bf16[256,256]{1,0:T(8,128)(2,1)S(1)} %constant_dynamic-update-slice_fusion), channel_id=1, source_target_pairs={{0,8},{1,9},{2,10},{3,11},{8,16},{9,17},{10,18},{11,19},{4,20},{5,... | collective-permute-start | bytes 393224 | tf_op jit(solution)/shard_map/ppermute | solution.py:232
  22.8 12.4 %all-to-all-start = ((bf16[4,384,256]{2,1,0:T(8,128)(2,1)}), bf16[4,384,256]{2,1,0:T(8,128)(2,1)S(1)}, u32[]{:S(2)}, u32[]{:S(2)}) async-start(bf16[4,384,256]{2,1,0:T(8,128)(2,1)} %broadcast_in_dim.3), calls=%async_computation | async-start | bytes 1572864 | tf_op jit(solution)/shard_map/all_to_all | solution.py:236
  26.8 35.1 %copy-start = (bf16[128,1024]{1,0:T(8,128)(2,1)S(1)}, bf16[128,1024]{1,0:T(8,128)(2,1)}, u32[]{:S(2)}) copy-start(bf16[128,1024]{1,0:T(8,128)(2,1)} %q_ref.1) | copy-start | bytes 786436
  26.8 15.1 %collective-permute-start.1 = (bf16[256,256]{1,0:T(8,128)(2,1)S(1)}, bf16[256,256]{1,0:T(8,128)(2,1)S(1)}, u32[]{:S(2)}, u32[]{:S(2)}) collective-permute-start(bf16[256,256]{1,0:T(8,128)(2,1)S(1)} %constant_dynamic-update-slice_fusion), channel_id=1, source_target_pairs={{0,24},{1,25},{2,26},{3,27},{8,32},{9,33},{10,34},{11,35},{4,36},{... | collective-permute-start | bytes 393224 | tf_op jit(solution)/shard_map/ppermute | solution.py:232
  35.2 32.5 %collective-permute-start.7 = (bf16[4,384,256]{2,1,0:T(8,128)(2,1)S(1)}, bf16[4,384,256]{2,1,0:T(8,128)(2,1)S(1)}, u32[]{:S(2)}, u32[]{:S(2)}) collective-permute-start(bf16[4,384,256]{2,1,0:T(8,128)(2,1)S(1)} %all-to-all-done.refs_0_), channel_id=1, source_target_pairs={{4,0},{5,1},{6,2},{7,3},{0,4},{1,5},{2,6},{3,7},{12,8},{13,9},{14,... | collective-permute-start | bytes 2359304 | tf_op jit(solution)/shard_map/ppermute | solution.py:232
  42.0 7.8 %collective-permute-start.2 = (bf16[256,256]{1,0:T(8,128)(2,1)S(1)}, bf16[256,256]{1,0:T(8,128)(2,1)S(1)}, u32[]{:S(2)}, u32[]{:S(2)}) collective-permute-start(bf16[256,256]{1,0:T(8,128)(2,1)S(1)} %collective-permute-done.1), channel_id=1, source_target_pairs={{1,0},{2,1},{3,2},{0,3},{5,4},{6,5},{7,6},{4,7},{9,8},{10,9},{11,1... | collective-permute-start | bytes 393224 | tf_op jit(solution)/shard_map/ppermute | solution.py:232
  44.8 6.9 %collective-permute-start.3 = (bf16[256,256]{1,0:T(8,128)(2,1)S(1)}, bf16[256,256]{1,0:T(8,128)(2,1)S(1)}, u32[]{:S(2)}, u32[]{:S(2)}) collective-permute-start(bf16[256,256]{1,0:T(8,128)(2,1)S(1)} %collective-permute-done.1), channel_id=1, source_target_pairs={{3,0},{0,1},{1,2},{2,3},{7,4},{4,5},{5,6},{6,7},{11,8},{8,9},{9,10... | collective-permute-start | bytes 393224 | tf_op jit(solution)/shard_map/ppermute | solution.py:232
  47.3 7.2 %collective-permute-start.4 = (bf16[256,256]{1,0:T(8,128)(2,1)S(1)}, bf16[256,256]{1,0:T(8,128)(2,1)S(1)}, u32[]{:S(2)}, u32[]{:S(2)}) collective-permute-start(bf16[256,256]{1,0:T(8,128)(2,1)S(1)} %collective-permute-done.1), channel_id=1, source_target_pairs={{2,0},{3,1},{0,2},{1,3},{6,4},{7,5},{4,6},{5,7},{10,8},{11,9},{8,1... | collective-permute-start | bytes 393224 | tf_op jit(solution)/shard_map/ppermute | solution.py:232
  54.5 7.4 %copy-start.1 = (s32[25]{0:T(128)S(1)}, s32[25]{0:T(128)}, u32[]{:S(2)}) copy-start(s32[25]{0:T(128)} %doc_ref.7) | copy-start | bytes 304
  54.5 26.5 %collective-permute-start.5 = (bf16[4,256,256]{2,1,0:T(8,128)(2,1)S(1)}, bf16[4,256,256]{2,1,0:T(8,128)(2,1)S(1)}, u32[]{:S(2)}, u32[]{:S(2)}) collective-permute-start(bf16[4,256,256]{2,1,0:T(8,128)(2,1)S(1)} %bitcast.2), channel_id=1, source_target_pairs={{4,0},{5,1},{6,2},{7,3},{0,4},{1,5},{2,6},{3,7},{12,8},{13,9},{14,... | collective-permute-start | bytes 1572872 | tf_op jit(solution)/shard_map/ppermute | solution.py:232

commit v2 on v1

--- a/solution.py
+++ b/solution.py
@@ -29,24 +29,58 @@
     return lax.fori_loop(0, doc_ref.shape[0], step, (jnp.int32(0), jnp.zeros_like(pos)), unroll=True)[1]
 
 
-def prepare_body(own, doc_ref, q_ref, query, row_start):
+def starts_body(own, doc_ref, row_start):
+    group, peer = own()
+    row_pos = (group * 4 + peer) * ROWS + lax.broadcasted_iota(jnp.int32, (8, ROWS), 1)
+    row_start[...] = starts_at(doc_ref, row_pos)
+
+
+def row_starts(doc_lengths, own):
+    return pl.pallas_call(
+        functools.partial(starts_body, own),
+        out_shape=pltpu.VMEM((8, ROWS), jnp.int32),
+        in_specs=[pl.BlockSpec(memory_space=pltpu.SMEM)],
+        out_specs=pl.BlockSpec(memory_space=pltpu.VMEM),
+        compiler_params=pltpu.CompilerParams(vmem_limit_bytes=4 << 20),
+    )(doc_lengths)
+
+
+def pairs_body(q_ref, query):
     for h in range(HEADS):
         rows = slice(h // 2 * WIDTH, (h // 2 + 1) * WIDTH)
         query[rows, h % 2 * ROWS : (h % 2 + 1) * ROWS] = q_ref[:, h * WIDTH : (h + 1) * WIDTH].T
-    group, peer = own()
-    row_pos = (group * 4 + peer) * ROWS + lax.broadcasted_iota(jnp.int32, (8, ROWS), 1)
-    row_start[...] = starts_at(doc_ref, row_pos)
-
-
-def prepare(doc_lengths, queries, own):
+
+
+def query_pairs(queries):
     vmem = pl.BlockSpec(memory_space=pltpu.VMEM)
     return pl.pallas_call(
-        functools.partial(prepare_body, own),
-        out_shape=(pltpu.VMEM((HEADS // 2 * WIDTH, 2 * ROWS), BF16), pltpu.VMEM((8, ROWS), jnp.int32)),
-        in_specs=[pl.BlockSpec(memory_space=pltpu.SMEM), vmem],
-        out_specs=(vmem, vmem),
+        pairs_body,
+        out_shape=pltpu.VMEM((HEADS // 2 * WIDTH, 2 * ROWS), BF16),
+        in_specs=[vmem],
+        out_specs=vmem,
         compiler_params=pltpu.CompilerParams(vmem_limit_bytes=4 << 20),
-    )(doc_lengths, queries)
+    )(queries)
+
+
+def spread_body(*refs):
+    out, at = refs[-1], 0
+    for ref in refs[:-1]:
+        value = ref[...]
+        for n in range(BLOCKS):
+            out[n, at : at + value.shape[0]] = value
+        at += value.shape[0]
+
+
+def spread(*values):
+    vmem = pl.BlockSpec(memory_space=pltpu.VMEM)
+    rows = sum(v.shape[0] for v in values)
+    return pl.pallas_call(
+        spread_body,
+        out_shape=pltpu.VMEM((BLOCKS, rows, 2 * WIDTH), BF16),
+        in_specs=[vmem] * len(values),
+        out_specs=vmem,
+        compiler_params=pltpu.CompilerParams(vmem_limit_bytes=4 << 20),
+    )(*(pltpu.with_memory_space_constraint(v, pltpu.VMEM) for v in values))
 
 
 def attend_body(first, last, places, own, doc_ref, query, start_ref, *refs):
@@ -232,16 +266,13 @@
     return lax.ppermute(value, AXES, pairs)
 
 
-def gathered(value):
-    return lax.all_to_all(jnp.broadcast_to(value, (BLOCKS, *value.shape)), "peer", 0, 0)
-
-
 def shards(queries, keys_values, doc_lengths):
     chip = jnp.concatenate([keys_values, moved(keys_values, lambda t: t ^ 4)], axis=0)
     pair_near = moved(chip, lambda t: t - 8 - 8 * (t // 4 % 2))
     pair_far = moved(chip, lambda t: t - 24 - 8 * (t // 4 % 2))
-    prepared = prepare(doc_lengths, queries, own)
-    near_mine = gathered(jnp.concatenate([keys_values, pair_near], axis=0))
+    starts = row_starts(doc_lengths, own)
+    prepared = query_pairs(queries), starts
+    near_mine = lax.all_to_all(spread(keys_values, pair_near), "peer", 0, 0)
     turns = []
     for k in (1, 3, 2):
         turns.append(moved(pair_far, lambda t, k=k: t // 4 * 4 + (t + k) % 4))

time: 85.8 us -> 85.8 us (level)
  Pallas kernels: 23.4 us -> 24.4 us
  local copies, waits for them, and re-layouts: 1.82 us -> 0.87 us
    pallas_call x1 -> x3, Pallas kernels: 0.66 us -> 1.65 us  [the longest x1 0.96 us: spread(): pl.pallas_call(spread_body, out_shape=pltpu.VMEM((BLOCKS, rows, 2 * WIDTH...]
    broadcast_in_dim x1 -> x0, local copies, waits for them, and re-layouts: 0.95 us -> none  [gathered(): jnp.broadcast_to(value, (BLOCKS, *value.shape))]
where the time goes in v2:
time: 85.8 us; the launch traced here: 85.4 us
  starting transfers between devices  36.3 us (42%)
  Pallas kernels  24.4 us (28%)
  waiting for transfers between devices  23 us (27%)
  local copies, waits for them, and re-layouts  0.87 us (1%)
    ppermute x8, starting transfers between devices, moved(): return lax.ppermute(value, AXES, pairs)  32.3 us
    pallas_call x3, Pallas kernels, attend(): pl.pallas_call(functools.partial(attend_body, state is None, last, places...  22.8 us
    ppermute x8, waiting for transfers between devices, moved(): return lax.ppermute(value, AXES, pairs)  16.6 us
    all_to_all x1, waiting for transfers between devices, shards(): near_mine = lax.all_to_all(spread(keys_values, pair_near), 'peer', 0, 0)  6.36 us
    all_to_all x1, starting transfers between devices, shards(): near_mine = lax.all_to_all(spread(keys_values, pair_near), 'peer', 0, 0)  4.01 us
  transfers between devices with their start and end apart: 9, of which 5 were waited for; matrix products, arithmetic and copies ran while one was open for 1% of the time, Pallas kernels for 22%

profile of v2, /device:TPU:49, one launch (start us, length us, event | category | flops | bytes accessed | tf_op | source)
XLA Modules:
  0.0 85.4 jit_solution(3788717136031824710)
XLA Ops:
  0.6 2.6 %collective-permute-start = (bf16[128,256]{1,0:T(8,128)(2,1)}, bf16[128,256]{1,0:T(8,128)(2,1)S(1)}, u32[]{:S(2)}, u32[]{:S(2)}) collective-permute-start(bf16[128,256]{1,0:T(8,128)(2,1)} %refs_0_.1), channel_id=1, source_target_pairs={{4,0},{5,1},{6,2},{7,3},{0,4},{1,5},{2,6},{3,7},{12,8},{13,9},{14,... | collective-permute-start | bytes 196616 | tf_op jit(solution)/shard_map/ppermute | solution.py:266
  3.2 0.8 constant_dynamic-update-slice_fusion.1
  4.1 0.0 copy-start.1
  4.1 0.2 collective-permute-done
  4.3 5.8 %collective-permute-start.6 = (bf16[256,256]{1,0:T(8,128)(2,1)S(1)}, bf16[256,256]{1,0:T(8,128)(2,1)S(1)}, u32[]{:S(2)}, u32[]{:S(2)}) collective-permute-start(bf16[256,256]{1,0:T(8,128)(2,1)S(1)} %constant_dynamic-update-slice_fusion), channel_id=1, source_target_pairs={{0,8},{1,9},{2,10},{3,11},{8,16},{9,17},{10,18},{11,19},{4,20},{5,... | collective-permute-start | bytes 393224 | tf_op jit(solution)/shard_map/ppermute | solution.py:266
  10.1 11.7 %collective-permute-done.6.refs_1_ = bf16[256,256]{1,0:T(8,128)(2,1)S(1)} collective-permute-done((bf16[256,256]{1,0:T(8,128)(2,1)S(1)}, bf16[256,256]{1,0:T(8,128)(2,1)S(1)}, u32[]{:S(2)}, u32[]{:S(2)}) %collective-permute-start.6) | collective-permute-done | bytes 131104 | tf_op jit(solution)/shard_map/ppermute | solution.py:266
  21.8 0.0 copy-done.1
  21.8 1.0 %shard_map.52 = bf16[4,384,256]{2,1,0:T(8,128)(2,1)} custom-call(bf16[128,256]{1,0:T(8,128)(2,1)S(1)} %copy-done.1, bf16[256,256]{1,0:T(8,128)(2,1)S(1)} %collective-permute-done.6.refs_1_), custom_call_target="tpu_custom_call" | custom-call | tf_op jit(solution)/shard_map/pallas_call | solution.py:77
  22.8 4.0 %all-to-all-start = ((bf16[4,384,256]{2,1,0:T(8,128)(2,1)}), bf16[4,384,256]{2,1,0:T(8,128)(2,1)S(1)}, u32[]{:S(2)}, u32[]{:S(2)}) async-start(bf16[4,384,256]{2,1,0:T(8,128)(2,1)} %shard_map.52), calls=%async_computation | async-start | bytes 1572864 | tf_op jit(solution)/shard_map/all_to_all | solution.py:275
  26.8 0.0 copy-start
  26.8 2.0 %collective-permute-start.1 = (bf16[256,256]{1,0:T(8,128)(2,1)S(1)}, bf16[256,256]{1,0:T(8,128)(2,1)S(1)}, u32[]{:S(2)}, u32[]{:S(2)}) collective-permute-start(bf16[256,256]{1,0:T(8,128)(2,1)S(1)} %constant_dynamic-update-slice_fusion), channel_id=1, source_target_pairs={{0,24},{1,25},{2,26},{3,27},{8,32},{9,33},{10,34},{11,35},{4,36},{... | collective-permute-start | bytes 393224 | tf_op jit(solution)/shard_map/ppermute | solution.py:266
  28.9 6.4 %all-to-all-done.refs_0_ = bf16[4,384,256]{2,1,0:T(8,128)(2,1)S(1)} async-done(((bf16[4,384,256]{2,1,0:T(8,128)(2,1)}), bf16[4,384,256]{2,1,0:T(8,128)(2,1)S(1)}, u32[]{:S(2)}, u32[]{:S(2)}) %all-to-all-start) | async-done | bytes 786464 | tf_op jit(solution)/shard_map/all_to_all | solution.py:275
  35.2 6.7 %collective-permute-start.7 = (bf16[4,384,256]{2,1,0:T(8,128)(2,1)S(1)}, bf16[4,384,256]{2,1,0:T(8,128)(2,1)S(1)}, u32[]{:S(2)}, u32[]{:S(2)}) collective-permute-start(bf16[4,384,256]{2,1,0:T(8,128)(2,1)S(1)} %all-to-all-done.refs_0_), channel_id=1, source_target_pairs={{4,0},{5,1},{6,2},{7,3},{0,4},{1,5},{2,6},{3,7},{12,8},{13,9},{14,... | collective-permute-start | bytes 2359304 | tf_op jit(solution)/shard_map/ppermute | solution.py:266
  42.0 0.0 collective-permute-done.1
  42.0 2.8 %collective-permute-start.2 = (bf16[256,256]{1,0:T(8,128)(2,1)S(1)}, bf16[256,256]{1,0:T(8,128)(2,1)S(1)}, u32[]{:S(2)}, u32[]{:S(2)}) collective-permute-start(bf16[256,256]{1,0:T(8,128)(2,1)S(1)} %collective-permute-done.1), channel_id=1, source_target_pairs={{1,0},{2,1},{3,2},{0,3},{5,4},{6,5},{7,6},{4,7},{9,8},{10,9},{11,1... | collective-permute-start | bytes 393224 | tf_op jit(solution)/shard_map/ppermute | solution.py:266
  44.8 2.5 %collective-permute-start.3 = (bf16[256,256]{1,0:T(8,128)(2,1)S(1)}, bf16[256,256]{1,0:T(8,128)(2,1)S(1)}, u32[]{:S(2)}, u32[]{:S(2)}) collective-permute-start(bf16[256,256]{1,0:T(8,128)(2,1)S(1)} %collective-permute-done.1), channel_id=1, source_target_pairs={{3,0},{0,1},{1,2},{2,3},{7,4},{4,5},{5,6},{6,7},{11,8},{8,9},{9,10... | collective-permute-start | bytes 393224 | tf_op jit(solution)/shard_map/ppermute | solution.py:266
  47.3 2.5 %collective-permute-start.4 = (bf16[256,256]{1,0:T(8,128)(2,1)S(1)}, bf16[256,256]{1,0:T(8,128)(2,1)S(1)}, u32[]{:S(2)}, u32[]{:S(2)}) collective-permute-start(bf16[256,256]{1,0:T(8,128)(2,1)S(1)} %collective-permute-done.1), channel_id=1, source_target_pairs={{2,0},{3,1},{0,2},{1,3},{6,4},{7,5},{4,6},{5,7},{10,8},{11,9},{8,1... | collective-permute-start | bytes 393224 | tf_op jit(solution)/shard_map/ppermute | solution.py:266
  49.8 0.0 collective-permute-done.2
  49.8 1.9 %collective-permute-done.3 = bf16[256,256]{1,0:T(8,128)(2,1)S(1)} collective-permute-done((bf16[256,256]{1,0:T(8,128)(2,1)S(1)}, bf16[256,256]{1,0:T(8,128)(2,1)S(1)}, u32[]{:S(2)}, u32[]{:S(2)}) %collective-permute-start.3) | collective-permute-done | bytes 131104 | tf_op jit(solution)/shard_map/ppermute | solution.py:266
  51.7 2.8 %collective-permute-done.4 = bf16[256,256]{1,0:T(8,128)(2,1)S(1)} collective-permute-done((bf16[256,256]{1,0:T(8,128)(2,1)S(1)}, bf16[256,256]{1,0:T(8,128)(2,1)S(1)}, u32[]{:S(2)}, u32[]{:S(2)}) %collective-permute-start.4) | collective-permute-done | bytes 131104 | tf_op jit(solution)/shard_map/ppermute | solution.py:266
  54.5 0.0 copy-start.2
  54.5 7.3 %collective-permute-start.5 = (bf16[4,256,256]{2,1,0:T(8,128)(2,1)S(1)}, bf16[4,256,256]{2,1,0:T(8,128)(2,1)S(1)}, u32[]{:S(2)}, u32[]{:S(2)}) collective-permute-start(bf16[4,256,256]{2,1,0:T(8,128)(2,1)S(1)} %bitcast.2), channel_id=1, source_target_pairs={{4,0},{5,1},{6,2},{7,3},{0,4},{1,5},{2,6},{3,7},{12,8},{13,9},{14,... | collective-permute-start | bytes 1572872 | tf_op jit(solution)/shard_map/ppermute | solution.py:266
  61.9 0.0 copy-done
  61.9 0.1 shard_map.50.query
  62.0 0.0 copy-done.2
  62.0 0.6 shard_map.51.start_ref
  62.6 5.1 %shard_map.53 = (f32[16,128]{1,0:T(8,128)S(1)}, f32[1024,128]{1,0:T(8,128)S(1)}) custom-call(s32[25]{0:T(128)S(1)} %copy-done.2, bf16[512,256]{1,0:T(8,128)(2,1)S(1)} %shard_map.50.query, s32[8,128]{1,0:T(8,128)S(1)} %shard_map.51.start_ref, bf16[4,384,256]{2,1,0:T(8,128)(2,1)S(1)} %all-to-all-done.refs_0_), custom_call_target="tpu_custom_call" | custom-call | tf_op jit(solution)/shard_map/pallas_call | solution.py:225
  67.7 0.0 collective-permute-done.7.refs_0_
  67.7 13.4 %shard_map.54 = (f32[16,128]{1,0:T(8,128)S(1)}, f32[1024,128]{1,0:T(8,128)S(1)}) custom-call(s32[25]{0:T(128)S(1)} %copy-done.2, bf16[512,256]{1,0:T(8,128)(2,1)S(1)} %shard_map.50.query, s32[8,128]{1,0:T(8,128)S(1)} %shard_map.51.start_ref, bf16[4,384,256]{2,1,0:T(8,128)(2,1)S(1)} %collective-permute-done.7.refs_0_, bf16[4,256,256]{2,1,0:T(8,128)(2,1)S(1)} %bitcast.3, ...), custom_call_target="tpu_custom_call" | custom-call | tf_op jit(solution)/shard_map/pallas_call | solution.py:225
  81.1 0.0 collective-permute-done.5.refs_0_
  81.1 4.3 %shard_map.55 = (bf16[128,1024]{1,0:T(8,128)(2,1)}, f32[8,128]{1,0:T(8,128)}) custom-call(s32[25]{0:T(128)S(1)} %copy-done.2, bf16[512,256]{1,0:T(8,128)(2,1)S(1)} %shard_map.50.query, s32[8,128]{1,0:T(8,128)S(1)} %shard_map.51.start_ref, bf16[4,256,256]{2,1,0:T(8,128)(2,1)S(1)} %collective-permute-done.5.refs_0_, f32[16,128]{1,0:T(8,128)S(1)} %get-tuple-element.10.refs_1_, ...), custom_call_target="tpu_custom_call" | custom-call | tf_op jit(solution)/shard_map/pallas_call | solution.py:225
  (2 shorter events, 0.0 us)
Async XLA Ops:
  0.6 3.7 %collective-permute-start = (bf16[128,256]{1,0:T(8,128)(2,1)}, bf16[128,256]{1,0:T(8,128)(2,1)S(1)}, u32[]{:S(2)}, u32[]{:S(2)}) collective-permute-start(bf16[128,256]{1,0:T(8,128)(2,1)} %refs_0_.1), channel_id=1, source_target_pairs={{4,0},{5,1},{6,2},{7,3},{0,4},{1,5},{2,6},{3,7},{12,8},{13,9},{14,... | collective-permute-start | bytes 196616 | tf_op jit(solution)/shard_map/ppermute | solution.py:266
  4.1 17.8 %copy-start.1 = (bf16[128,256]{1,0:T(8,128)(2,1)S(1)}, bf16[128,256]{1,0:T(8,128)(2,1)}, u32[]{:S(2)}) copy-start(bf16[128,256]{1,0:T(8,128)(2,1)} %refs_0_.1) | copy-start | bytes 196612
  4.3 17.5 %collective-permute-start.6 = (bf16[256,256]{1,0:T(8,128)(2,1)S(1)}, bf16[256,256]{1,0:T(8,128)(2,1)S(1)}, u32[]{:S(2)}, u32[]{:S(2)}) collective-permute-start(bf16[256,256]{1,0:T(8,128)(2,1)S(1)} %constant_dynamic-update-slice_fusion), channel_id=1, source_target_pairs={{0,8},{1,9},{2,10},{3,11},{8,16},{9,17},{10,18},{11,19},{4,20},{5,... | collective-permute-start | bytes 393224 | tf_op jit(solution)/shard_map/ppermute | solution.py:266
  22.8 12.4 %all-to-all-start = ((bf16[4,384,256]{2,1,0:T(8,128)(2,1)}), bf16[4,384,256]{2,1,0:T(8,128)(2,1)S(1)}, u32[]{:S(2)}, u32[]{:S(2)}) async-start(bf16[4,384,256]{2,1,0:T(8,128)(2,1)} %shard_map.52), calls=%async_computation | async-start | bytes 1572864 | tf_op jit(solution)/shard_map/all_to_all | solution.py:275
  26.8 35.1 %copy-start = (bf16[128,1024]{1,0:T(8,128)(2,1)S(1)}, bf16[128,1024]{1,0:T(8,128)(2,1)}, u32[]{:S(2)}) copy-start(bf16[128,1024]{1,0:T(8,128)(2,1)} %q_ref.1) | copy-start | bytes 786436
  26.8 15.1 %collective-permute-start.1 = (bf16[256,256]{1,0:T(8,128)(2,1)S(1)}, bf16[256,256]{1,0:T(8,128)(2,1)S(1)}, u32[]{:S(2)}, u32[]{:S(2)}) collective-permute-start(bf16[256,256]{1,0:T(8,128)(2,1)S(1)} %constant_dynamic-update-slice_fusion), channel_id=1, source_target_pairs={{0,24},{1,25},{2,26},{3,27},{8,32},{9,33},{10,34},{11,35},{4,36},{... | collective-permute-start | bytes 393224 | tf_op jit(solution)/shard_map/ppermute | solution.py:266
  35.2 32.5 %collective-permute-start.7 = (bf16[4,384,256]{2,1,0:T(8,128)(2,1)S(1)}, bf16[4,384,256]{2,1,0:T(8,128)(2,1)S(1)}, u32[]{:S(2)}, u32[]{:S(2)}) collective-permute-start(bf16[4,384,256]{2,1,0:T(8,128)(2,1)S(1)} %all-to-all-done.refs_0_), channel_id=1, source_target_pairs={{4,0},{5,1},{6,2},{7,3},{0,4},{1,5},{2,6},{3,7},{12,8},{13,9},{14,... | collective-permute-start | bytes 2359304 | tf_op jit(solution)/shard_map/ppermute | solution.py:266
  42.0 7.8 %collective-permute-start.2 = (bf16[256,256]{1,0:T(8,128)(2,1)S(1)}, bf16[256,256]{1,0:T(8,128)(2,1)S(1)}, u32[]{:S(2)}, u32[]{:S(2)}) collective-permute-start(bf16[256,256]{1,0:T(8,128)(2,1)S(1)} %collective-permute-done.1), channel_id=1, source_target_pairs={{1,0},{2,1},{3,2},{0,3},{5,4},{6,5},{7,6},{4,7},{9,8},{10,9},{11,1... | collective-permute-start | bytes 393224 | tf_op jit(solution)/shard_map/ppermute | solution.py:266
  44.8 6.9 %collective-permute-start.3 = (bf16[256,256]{1,0:T(8,128)(2,1)S(1)}, bf16[256,256]{1,0:T(8,128)(2,1)S(1)}, u32[]{:S(2)}, u32[]{:S(2)}) collective-permute-start(bf16[256,256]{1,0:T(8,128)(2,1)S(1)} %collective-permute-done.1), channel_id=1, source_target_pairs={{3,0},{0,1},{1,2},{2,3},{7,4},{4,5},{5,6},{6,7},{11,8},{8,9},{9,10... | collective-permute-start | bytes 393224 | tf_op jit(solution)/shard_map/ppermute | solution.py:266
  47.3 7.2 %collective-permute-start.4 = (bf16[256,256]{1,0:T(8,128)(2,1)S(1)}, bf16[256,256]{1,0:T(8,128)(2,1)S(1)}, u32[]{:S(2)}, u32[]{:S(2)}) collective-permute-start(bf16[256,256]{1,0:T(8,128)(2,1)S(1)} %collective-permute-done.1), channel_id=1, source_target_pairs={{2,0},{3,1},{0,2},{1,3},{6,4},{7,5},{4,6},{5,7},{10,8},{11,9},{8,1... | collective-permute-start | bytes 393224 | tf_op jit(solution)/shard_map/ppermute | solution.py:266
  54.5 7.5 %copy-start.2 = (s32[25]{0:T(128)S(1)}, s32[25]{0:T(128)}, u32[]{:S(2)}) copy-start(s32[25]{0:T(128)} %doc_ref.7) | copy-start | bytes 304
  54.5 26.6 %collective-permute-start.5 = (bf16[4,256,256]{2,1,0:T(8,128)(2,1)S(1)}, bf16[4,256,256]{2,1,0:T(8,128)(2,1)S(1)}, u32[]{:S(2)}, u32[]{:S(2)}) collective-permute-start(bf16[4,256,256]{2,1,0:T(8,128)(2,1)S(1)} %bitcast.2), channel_id=1, source_target_pairs={{4,0},{5,1},{6,2},{7,3},{0,4},{1,5},{2,6},{3,7},{12,8},{13,9},{14,... | collective-permute-start | bytes 1572872 | tf_op jit(solution)/shard_map/ppermute | solution.py:266

commit v3 on v2

--- a/solution.py
+++ b/solution.py
@@ -13,6 +13,7 @@
 HEADS = 8
 WIDTH = 128
 BLOCKS = 4
+CHUNK = 256
 NEG = -1e30
 LIMIT = 2.0**40
 SCALE = math.log2(math.e) / math.sqrt(WIDTH)
@@ -141,10 +142,16 @@
         for p in range(HEADS // 2):
             h = 2 * p
             held = pair_rows(stat, h)
-            score = jnp.dot(keys, query[p * WIDTH : (p + 1) * WIDTH], preferred_element_type=F32) * F32(SCALE) - held
-            if masked:
-                score = score + bias[...]
-            part = jnp.dot(values, jnp.exp2(score).astype(BF16), preferred_element_type=F32)
+            part = None
+            for c in range(0, span, CHUNK):
+                score = jnp.dot(
+                    keys[c : c + CHUNK], query[p * WIDTH : (p + 1) * WIDTH], preferred_element_type=F32
+                ) * F32(SCALE) - held
+                if masked:
+                    score = score + bias[c : c + CHUNK]
+                weight = jnp.exp2(score).astype(BF16)
+                piece = jnp.dot(values[:, c : c + CHUNK], weight, preferred_element_type=F32)
+                part = piece if part is None else part + piece
             for k in range(2):
                 rows, cols = slice((h + k) * WIDTH, (h + k + 1) * WIDTH), slice(k * ROWS, (k + 1) * ROWS)
                 acc[rows] += part[:WIDTH, cols]
@@ -236,24 +243,20 @@
 TURNS = (0, 1, 3, 2)
 
 
-def tiles(of_other, groups, turned=False):
+def tiles(of_other, back, turned=False):
     def at(kv_ref, i, group):
         def load():
             return kv_ref[:, pl.ds(pl.multiple_of(i * ROWS, ROWS), ROWS), :].reshape(BLOCKS * ROWS, 2 * WIDTH)
 
         line, core = group // 2, group % 2
-        return load, groups(i, line, 1 - core if of_other else core), TURNS if turned else range(BLOCKS)
+        if of_other:
+            core = 1 - core
+        order = TURNS if turned else range(BLOCKS)
+        if not back:
+            return load, 2 * line + core, order
+        return load, 2 * (line - back - core) + jnp.where(i == 0, core, 1 - core), order
 
     return at
-
-
-def near(i, line, core):
-    pair = 2 * (line - 1 - core) + jnp.where(i == 1, core, 1 - core)
-    return jnp.where(i == 0, 2 * line + core, pair)
-
-
-def far(i, line, core):
-    return 2 * (line - 3 - core) + jnp.where(i == 0, core, 1 - core)
 
 
 def own():
@@ -266,24 +269,37 @@
     return lax.ppermute(value, AXES, pairs)
 
 
+def across(value):
+    return lax.all_to_all(value, "peer", 0, 0)
+
+
+def swapped(value):
+    return moved(value, lambda t: t ^ 4)
+
+
 def shards(queries, keys_values, doc_lengths):
-    chip = jnp.concatenate([keys_values, moved(keys_values, lambda t: t ^ 4)], axis=0)
+    chip = jnp.concatenate([keys_values, swapped(keys_values)], axis=0)
     pair_near = moved(chip, lambda t: t - 8 - 8 * (t // 4 % 2))
+    own_mine = across(spread(keys_values))
+    own_other = swapped(own_mine)
     pair_far = moved(chip, lambda t: t - 24 - 8 * (t // 4 % 2))
     starts = row_starts(doc_lengths, own)
     prepared = query_pairs(queries), starts
-    near_mine = lax.all_to_all(spread(keys_values, pair_near), "peer", 0, 0)
+
+    def step(pieces, state, last=False):
+        return attend(doc_lengths, prepared, pieces, state, last, own)
+
+    state = step([(own_mine, tiles(False, 0)), (own_other, tiles(True, 0))], None)
+    near_mine = across(spread(pair_near))
     turns = []
     for k in (1, 3, 2):
         turns.append(moved(pair_far, lambda t, k=k: t // 4 * 4 + (t + k) % 4))
     far_mine = jnp.concatenate([pair_far, *turns], axis=0).reshape(BLOCKS, *pair_far.shape)
-    near_other = moved(near_mine, lambda t: t ^ 4)
-    far_other = moved(far_mine, lambda t: t ^ 4)
-    state = attend(doc_lengths, prepared, [(near_mine, tiles(False, near))], None, False, own)
-    state = attend(
-        doc_lengths, prepared, [(near_other, tiles(True, near)), (far_mine, tiles(False, far, True))], state, False, own
-    )
-    attended, log_total = attend(doc_lengths, prepared, [(far_other, tiles(True, far, True))], state, True, own)
+    near_other = swapped(near_mine)
+    state = step([(near_mine, tiles(False, 1))], state)
+    far_other = swapped(far_mine)
+    state = step([(near_other, tiles(True, 1)), (far_mine, tiles(False, 3, True))], state)
+    attended, log_total = step([(far_other, tiles(True, 3, True))], state, True)
     return attended, log_total.T
 
 

time: 85.8 us -> 97.1 us (1.13)
  blocking collectives: 0 us -> 10.6 us
  starting transfers between devices: 36.3 us -> 41.2 us
  Pallas kernels: 24.4 us -> 21.3 us
  waiting for transfers between devices: 23 us -> 21.7 us
    all_to_all x0 -> x1, blocking collectives: none -> 10.6 us  [across(): return lax.all_to_all(value, 'peer', 0, 0)]
    all_to_all x1, waiting for transfers between devices: 6.36 us -> 0.01 us  [across(): return lax.all_to_all(value, 'peer', 0, 0)]
    ppermute x8 -> x9, waiting for transfers between devices: 16.6 us -> 21.7 us  [moved(): return lax.ppermute(value, AXES, pairs)]
    ppermute x8 -> x9, starting transfers between devices: 32.3 us -> 37.2 us  [moved(): return lax.ppermute(value, AXES, pairs)]
    pallas_call x3 -> x4, Pallas kernels: 22.8 us -> 19.8 us  [attend(): pl.pallas_call(functools.partial(attend_body, state is None, last, places...]
  transfers between devices with their start and end apart: 9 -> 10, of which waited for: 5 -> 4; matrix products, arithmetic and copies ran while one was open for 1% -> 1% of each run, Pallas kernels for 22% -> 17%
where the time goes in v3:
time: 97.1 us; the launch traced here: 96.6 us
  starting transfers between devices  41.2 us (42%)
  waiting for transfers between devices  21.7 us (22%)
  Pallas kernels  21.3 us (22%)
  blocking collectives  10.6 us (11%)
    ppermute x9, starting transfers between devices, moved(): return lax.ppermute(value, AXES, pairs)  37.2 us
    ppermute x9, waiting for transfers between devices, moved(): return lax.ppermute(value, AXES, pairs)  21.7 us
    pallas_call x4, Pallas kernels, attend(): pl.pallas_call(functools.partial(attend_body, state is None, last, places...  19.8 us
    all_to_all x1, blocking collectives, across(): return lax.all_to_all(value, 'peer', 0, 0)  10.6 us
    all_to_all x1, starting transfers between devices, across(): return lax.all_to_all(value, 'peer', 0, 0)  4.01 us
  transfers between devices with their start and end apart: 10, of which 4 were waited for; matrix products, arithmetic and copies ran while one was open for 1% of the time, Pallas kernels for 17%

profile of v3, /device:TPU:49, one launch (start us, length us, event | category | flops | bytes accessed | tf_op | source)
XLA Modules:
  0.0 96.6 jit_solution(14731805397290391242)
XLA Ops:
  0.6 2.6 %collective-permute-start = (bf16[128,256]{1,0:T(8,128)(2,1)}, bf16[128,256]{1,0:T(8,128)(2,1)S(1)}, u32[]{:S(2)}, u32[]{:S(2)}) collective-permute-start(bf16[128,256]{1,0:T(8,128)(2,1)} %refs_0_.1), channel_id=1, source_target_pairs={{4,0},{5,1},{6,2},{7,3},{0,4},{1,5},{2,6},{3,7},{12,8},{13,9},{14,... | collective-permute-start | bytes 196616 | tf_op jit(solution)/shard_map/ppermute | solution.py:269
  3.2 0.8 constant_dynamic-update-slice_fusion.1
  4.1 0.2 collective-permute-done
  4.3 5.8 %collective-permute-start.6 = (bf16[256,256]{1,0:T(8,128)(2,1)S(1)}, bf16[256,256]{1,0:T(8,128)(2,1)S(1)}, u32[]{:S(2)}, u32[]{:S(2)}) collective-permute-start(bf16[256,256]{1,0:T(8,128)(2,1)S(1)} %constant_dynamic-update-slice_fusion), channel_id=1, source_target_pairs={{0,8},{1,9},{2,10},{3,11},{8,16},{9,17},{10,18},{11,19},{4,20},{5,... | collective-permute-start | bytes 393224 | tf_op jit(solution)/shard_map/ppermute | solution.py:269
  10.1 11.7 %collective-permute-done.6.refs_0_ = bf16[256,256]{1,0:T(8,128)(2,1)S(1)} collective-permute-done((bf16[256,256]{1,0:T(8,128)(2,1)S(1)}, bf16[256,256]{1,0:T(8,128)(2,1)S(1)}, u32[]{:S(2)}, u32[]{:S(2)}) %collective-permute-start.6) | collective-permute-done | bytes 131104 | tf_op jit(solution)/shard_map/ppermute | solution.py:269
  21.8 0.8 shard_map.52
  22.7 4.0 %all-to-all-start = ((bf16[4,256,256]{2,1,0:T(8,128)(2,1)}), bf16[4,256,256]{2,1,0:T(8,128)(2,1)S(1)}, u32[]{:S(2)}, u32[]{:S(2)}) async-start(bf16[4,256,256]{2,1,0:T(8,128)(2,1)} %shard_map.52), calls=%async_computation | async-start | bytes 1048576 | tf_op jit(solution)/shard_map/all_to_all | solution.py:273
  26.7 0.0 copy-start
  26.7 2.0 %collective-permute-start.1 = (bf16[256,256]{1,0:T(8,128)(2,1)S(1)}, bf16[256,256]{1,0:T(8,128)(2,1)S(1)}, u32[]{:S(2)}, u32[]{:S(2)}) collective-permute-start(bf16[256,256]{1,0:T(8,128)(2,1)S(1)} %constant_dynamic-update-slice_fusion), channel_id=1, source_target_pairs={{0,24},{1,25},{2,26},{3,27},{8,32},{9,33},{10,34},{11,35},{4,36},{... | collective-permute-start | bytes 393224 | tf_op jit(solution)/shard_map/ppermute | solution.py:269
  28.7 9.3 %collective-permute-done.1 = bf16[256,256]{1,0:T(8,128)(2,1)S(1)} collective-permute-done((bf16[256,256]{1,0:T(8,128)(2,1)S(1)}, bf16[256,256]{1,0:T(8,128)(2,1)S(1)}, u32[]{:S(2)}, u32[]{:S(2)}) %collective-permute-start.1) | collective-permute-done | bytes 131104 | tf_op jit(solution)/shard_map/ppermute | solution.py:269
  38.0 4.3 %collective-permute-start.2 = (bf16[256,256]{1,0:T(8,128)(2,1)S(1)}, bf16[256,256]{1,0:T(8,128)(2,1)S(1)}, u32[]{:S(2)}, u32[]{:S(2)}) collective-permute-start(bf16[256,256]{1,0:T(8,128)(2,1)S(1)} %collective-permute-done.1), channel_id=1, source_target_pairs={{1,0},{2,1},{3,2},{0,3},{5,4},{6,5},{7,6},{4,7},{9,8},{10,9},{11,1... | collective-permute-start | bytes 393224 | tf_op jit(solution)/shard_map/ppermute | solution.py:269
  42.3 1.9 %collective-permute-start.3 = (bf16[256,256]{1,0:T(8,128)(2,1)S(1)}, bf16[256,256]{1,0:T(8,128)(2,1)S(1)}, u32[]{:S(2)}, u32[]{:S(2)}) collective-permute-start(bf16[256,256]{1,0:T(8,128)(2,1)S(1)} %collective-permute-done.1), channel_id=1, source_target_pairs={{3,0},{0,1},{1,2},{2,3},{7,4},{4,5},{5,6},{6,7},{11,8},{8,9},{9,10... | collective-permute-start | bytes 393224 | tf_op jit(solution)/shard_map/ppermute | solution.py:269
  44.2 3.7 %collective-permute-start.4 = (bf16[256,256]{1,0:T(8,128)(2,1)S(1)}, bf16[256,256]{1,0:T(8,128)(2,1)S(1)}, u32[]{:S(2)}, u32[]{:S(2)}) collective-permute-start(bf16[256,256]{1,0:T(8,128)(2,1)S(1)} %collective-permute-done.1), channel_id=1, source_target_pairs={{2,0},{3,1},{0,2},{1,3},{6,4},{7,5},{4,6},{5,7},{10,8},{11,9},{8,1... | collective-permute-start | bytes 393224 | tf_op jit(solution)/shard_map/ppermute | solution.py:269
  47.9 0.0 all-to-all-done.refs_0_
  47.9 9.6 %collective-permute-start.7 = (bf16[4,256,256]{2,1,0:T(8,128)(2,1)S(1)}, bf16[4,256,256]{2,1,0:T(8,128)(2,1)S(1)}, u32[]{:S(2)}, u32[]{:S(2)}) collective-permute-start(bf16[4,256,256]{2,1,0:T(8,128)(2,1)S(1)} %all-to-all-done.refs_0_), channel_id=1, source_target_pairs={{4,0},{5,1},{6,2},{7,3},{0,4},{1,5},{2,6},{3,7},{12,8},{13,9},{14,... | collective-permute-start | bytes 1572872 | tf_op jit(solution)/shard_map/ppermute | solution.py:269
  57.6 0.0 collective-permute-done.2
  57.6 0.0 collective-permute-done.3
  57.6 0.0 collective-permute-done.4
  57.6 4.1 %collective-permute-start.5 = (bf16[4,256,256]{2,1,0:T(8,128)(2,1)S(1)}, bf16[4,256,256]{2,1,0:T(8,128)(2,1)S(1)}, u32[]{:S(2)}, u32[]{:S(2)}) collective-permute-start(bf16[4,256,256]{2,1,0:T(8,128)(2,1)S(1)} %bitcast.2), channel_id=1, source_target_pairs={{4,0},{5,1},{6,2},{7,3},{0,4},{1,5},{2,6},{3,7},{12,8},{13,9},{14,... | collective-permute-start | bytes 1572872 | tf_op jit(solution)/shard_map/ppermute | solution.py:269
  61.7 0.0 copy-done
  61.8 0.0 copy-start.1
  61.8 10.6 %all_to_all.10.refs_0_ = bf16[4,128,256]{2,1,0:T(8,128)(2,1)S(1)} all-to-all(bf16[4,128,256]{2,1,0:T(8,128)(2,1)S(1)} %shard_map.53), channel_id=1, replica_groups=mesh['group'=192,'peer'=4] {'peer'}, dimensions={0} | all-to-all | bytes 524288 | tf_op jit(solution)/shard_map/all_to_all | solution.py:273
  72.4 0.0 copy-start.2
  72.4 3.2 %collective-permute-start.8 = (bf16[4,128,256]{2,1,0:T(8,128)(2,1)S(1)}, bf16[4,128,256]{2,1,0:T(8,128)(2,1)S(1)}, u32[]{:S(2)}, u32[]{:S(2)}) collective-permute-start(bf16[4,128,256]{2,1,0:T(8,128)(2,1)S(1)} %all_to_all.10.refs_0_), channel_id=1, source_target_pairs={{4,0},{5,1},{6,2},{7,3},{0,4},{1,5},{2,6},{3,7},{12,8},{13,9},{14,... | collective-permute-start | bytes 786440 | tf_op jit(solution)/shard_map/ppermute | solution.py:269
  75.6 0.0 copy-done.1
  75.6 0.1 shard_map.50.query
  75.7 0.0 copy-done.2
  75.7 0.6 shard_map.51.start_ref
  76.3 0.4 collective-permute-done.8.refs_1_
  76.7 3.5 %shard_map.54 = (f32[16,128]{1,0:T(8,128)S(1)}, f32[1024,128]{1,0:T(8,128)S(1)}) custom-call(s32[25]{0:T(128)S(1)} %copy-done.2, bf16[512,256]{1,0:T(8,128)(2,1)S(1)} %shard_map.50.query, s32[8,128]{1,0:T(8,128)S(1)} %shard_map.51.start_ref, bf16[4,128,256]{2,1,0:T(8,128)(2,1)S(1)} %all_to_all.10.refs_0_, bf16[4,128,256]{2,1,0:T(8,128)(2,1)S(1)} %collective-permute-done.8.refs_1_), custom_call_target="tpu_custom_call" | custom-call | tf_op jit(solution)/shard_map/pallas_call | solution.py:232
  80.2 3.1 %shard_map.55 = (f32[16,128]{1,0:T(8,128)S(1)}, f32[1024,128]{1,0:T(8,128)S(1)}) custom-call(s32[25]{0:T(128)S(1)} %copy-done.2, bf16[512,256]{1,0:T(8,128)(2,1)S(1)} %shard_map.50.query, s32[8,128]{1,0:T(8,128)S(1)} %shard_map.51.start_ref, bf16[4,256,256]{2,1,0:T(8,128)(2,1)S(1)} %all-to-all-done.refs_0_, f32[16,128]{1,0:T(8,128)S(1)} %get-tuple-element.10.refs_1_, ...), custom_call_target="tpu_custom_call" | custom-call | tf_op jit(solution)/shard_map/pallas_call | solution.py:232
  83.4 0.0 collective-permute-done.7.refs_0_
  83.4 9.4 %shard_map.56 = (f32[16,128]{1,0:T(8,128)S(1)}, f32[1024,128]{1,0:T(8,128)S(1)}) custom-call(s32[25]{0:T(128)S(1)} %copy-done.2, bf16[512,256]{1,0:T(8,128)(2,1)S(1)} %shard_map.50.query, s32[8,128]{1,0:T(8,128)S(1)} %shard_map.51.start_ref, bf16[4,256,256]{2,1,0:T(8,128)(2,1)S(1)} %collective-permute-done.7.refs_0_, bf16[4,256,256]{2,1,0:T(8,128)(2,1)S(1)} %bitcast.3, ...), custom_call_target="tpu_custom_call" | custom-call | tf_op jit(solution)/shard_map/pallas_call | solution.py:232
  92.7 0.0 collective-permute-done.5.refs_0_
  92.8 3.8 %shard_map.57 = (bf16[128,1024]{1,0:T(8,128)(2,1)}, f32[8,128]{1,0:T(8,128)}) custom-call(s32[25]{0:T(128)S(1)} %copy-done.2, bf16[512,256]{1,0:T(8,128)(2,1)S(1)} %shard_map.50.query, s32[8,128]{1,0:T(8,128)S(1)} %shard_map.51.start_ref, bf16[4,256,256]{2,1,0:T(8,128)(2,1)S(1)} %collective-permute-done.5.refs_0_, f32[16,128]{1,0:T(8,128)S(1)} %get-tuple-element.14.refs_1_, ...), custom_call_target="tpu_custom_call" | custom-call | tf_op jit(solution)/shard_map/pallas_call | solution.py:232
  (3 shorter events, 0.1 us)
Async XLA Ops:
  0.6 3.7 %collective-permute-start = (bf16[128,256]{1,0:T(8,128)(2,1)}, bf16[128,256]{1,0:T(8,128)(2,1)S(1)}, u32[]{:S(2)}, u32[]{:S(2)}) collective-permute-start(bf16[128,256]{1,0:T(8,128)(2,1)} %refs_0_.1), channel_id=1, source_target_pairs={{4,0},{5,1},{6,2},{7,3},{0,4},{1,5},{2,6},{3,7},{12,8},{13,9},{14,... | collective-permute-start | bytes 196616 | tf_op jit(solution)/shard_map/ppermute | solution.py:269
  4.3 17.5 %collective-permute-start.6 = (bf16[256,256]{1,0:T(8,128)(2,1)S(1)}, bf16[256,256]{1,0:T(8,128)(2,1)S(1)}, u32[]{:S(2)}, u32[]{:S(2)}) collective-permute-start(bf16[256,256]{1,0:T(8,128)(2,1)S(1)} %constant_dynamic-update-slice_fusion), channel_id=1, source_target_pairs={{0,8},{1,9},{2,10},{3,11},{8,16},{9,17},{10,18},{11,19},{4,20},{5,... | collective-permute-start | bytes 393224 | tf_op jit(solution)/shard_map/ppermute | solution.py:269
  22.7 25.2 %all-to-all-start = ((bf16[4,256,256]{2,1,0:T(8,128)(2,1)}), bf16[4,256,256]{2,1,0:T(8,128)(2,1)S(1)}, u32[]{:S(2)}, u32[]{:S(2)}) async-start(bf16[4,256,256]{2,1,0:T(8,128)(2,1)} %shard_map.52), calls=%async_computation | async-start | bytes 1048576 | tf_op jit(solution)/shard_map/all_to_all | solution.py:273
  26.7 35.1 %copy-start = (bf16[128,256]{1,0:T(8,128)(2,1)S(1)}, bf16[128,256]{1,0:T(8,128)(2,1)}, u32[]{:S(2)}) copy-start(bf16[128,256]{1,0:T(8,128)(2,1)} %refs_0_.1) | copy-start | bytes 196612
  26.7 11.3 %collective-permute-start.1 = (bf16[256,256]{1,0:T(8,128)(2,1)S(1)}, bf16[256,256]{1,0:T(8,128)(2,1)S(1)}, u32[]{:S(2)}, u32[]{:S(2)}) collective-permute-start(bf16[256,256]{1,0:T(8,128)(2,1)S(1)} %constant_dynamic-update-slice_fusion), channel_id=1, source_target_pairs={{0,24},{1,25},{2,26},{3,27},{8,32},{9,33},{10,34},{11,35},{4,36},{... | collective-permute-start | bytes 393224 | tf_op jit(solution)/shard_map/ppermute | solution.py:269
  38.0 19.6 %collective-permute-start.2 = (bf16[256,256]{1,0:T(8,128)(2,1)S(1)}, bf16[256,256]{1,0:T(8,128)(2,1)S(1)}, u32[]{:S(2)}, u32[]{:S(2)}) collective-permute-start(bf16[256,256]{1,0:T(8,128)(2,1)S(1)} %collective-permute-done.1), channel_id=1, source_target_pairs={{1,0},{2,1},{3,2},{0,3},{5,4},{6,5},{7,6},{4,7},{9,8},{10,9},{11,1... | collective-permute-start | bytes 393224 | tf_op jit(solution)/shard_map/ppermute | solution.py:269
  42.3 15.3 %collective-permute-start.3 = (bf16[256,256]{1,0:T(8,128)(2,1)S(1)}, bf16[256,256]{1,0:T(8,128)(2,1)S(1)}, u32[]{:S(2)}, u32[]{:S(2)}) collective-permute-start(bf16[256,256]{1,0:T(8,128)(2,1)S(1)} %collective-permute-done.1), channel_id=1, source_target_pairs={{3,0},{0,1},{1,2},{2,3},{7,4},{4,5},{5,6},{6,7},{11,8},{8,9},{9,10... | collective-permute-start | bytes 393224 | tf_op jit(solution)/shard_map/ppermute | solution.py:269
  44.2 13.3 %collective-permute-start.4 = (bf16[256,256]{1,0:T(8,128)(2,1)S(1)}, bf16[256,256]{1,0:T(8,128)(2,1)S(1)}, u32[]{:S(2)}, u32[]{:S(2)}) collective-permute-start(bf16[256,256]{1,0:T(8,128)(2,1)S(1)} %collective-permute-done.1), channel_id=1, source_target_pairs={{2,0},{3,1},{0,2},{1,3},{6,4},{7,5},{4,6},{5,7},{10,8},{11,9},{8,1... | collective-permute-start | bytes 393224 | tf_op jit(solution)/shard_map/ppermute | solution.py:269
  47.9 35.5 %collective-permute-start.7 = (bf16[4,256,256]{2,1,0:T(8,128)(2,1)S(1)}, bf16[4,256,256]{2,1,0:T(8,128)(2,1)S(1)}, u32[]{:S(2)}, u32[]{:S(2)}) collective-permute-start(bf16[4,256,256]{2,1,0:T(8,128)(2,1)S(1)} %all-to-all-done.refs_0_), channel_id=1, source_target_pairs={{4,0},{5,1},{6,2},{7,3},{0,4},{1,5},{2,6},{3,7},{12,8},{13,9},{14,... | collective-permute-start | bytes 1572872 | tf_op jit(solution)/shard_map/ppermute | solution.py:269
  57.6 35.1 %collective-permute-start.5 = (bf16[4,256,256]{2,1,0:T(8,128)(2,1)S(1)}, bf16[4,256,256]{2,1,0:T(8,128)(2,1)S(1)}, u32[]{:S(2)}, u32[]{:S(2)}) collective-permute-start(bf16[4,256,256]{2,1,0:T(8,128)(2,1)S(1)} %bitcast.2), channel_id=1, source_target_pairs={{4,0},{5,1},{6,2},{7,3},{0,4},{1,5},{2,6},{3,7},{12,8},{13,9},{14,... | collective-permute-start | bytes 1572872 | tf_op jit(solution)/shard_map/ppermute | solution.py:269
  61.8 13.8 %copy-start.1 = (bf16[128,1024]{1,0:T(8,128)(2,1)S(1)}, bf16[128,1024]{1,0:T(8,128)(2,1)}, u32[]{:S(2)}) copy-start(bf16[128,1024]{1,0:T(8,128)(2,1)} %q_ref.1) | copy-start | bytes 786436
  72.4 3.3 %copy-start.2 = (s32[25]{0:T(128)S(1)}, s32[25]{0:T(128)}, u32[]{:S(2)}) copy-start(s32[25]{0:T(128)} %doc_ref.9) | copy-start | bytes 304
  72.4 4.3 %collective-permute-start.8 = (bf16[4,128,256]{2,1,0:T(8,128)(2,1)S(1)}, bf16[4,128,256]{2,1,0:T(8,128)(2,1)S(1)}, u32[]{:S(2)}, u32[]{:S(2)}) collective-permute-start(bf16[4,128,256]{2,1,0:T(8,128)(2,1)S(1)} %all_to_all.10.refs_0_), channel_id=1, source_target_pairs={{4,0},{5,1},{6,2},{7,3},{0,4},{1,5},{2,6},{3,7},{12,8},{13,9},{14,... | collective-permute-start | bytes 786440 | tf_op jit(solution)/shard_map/ppermute | solution.py:269

commit v4 on v3

--- a/solution.py
+++ b/solution.py
@@ -108,18 +108,15 @@
         values = jnp.concatenate([tile[:, WIDTH:].T, jnp.ones((16, span), BF16)], axis=0)
         return tile[:, :WIDTH], values
 
-    def set_bias(base, order):
-        for n, place in enumerate(order):
-            if not isinstance(order, range):
-                place = (peer + place) % BLOCKS
-            key_pos = base + place * ROWS + lax.broadcasted_iota(jnp.int32, (ROWS, ROWS), 0)
-            hidden = jnp.where((key_pos >= row_start) & (key_pos <= row_pos), F32(0), F32(NEG))
-            bias[n * ROWS : (n + 1) * ROWS, :ROWS] = hidden
-            bias[n * ROWS : (n + 1) * ROWS, ROWS:] = hidden
-
-    def exact(tile, base, order):
+    def set_bias(base):
+        key_pos = base + lax.broadcasted_iota(jnp.int32, (span, ROWS), 0)
+        hidden = jnp.where((key_pos >= row_start) & (key_pos <= row_pos), F32(0), F32(NEG))
+        bias[:, :ROWS] = hidden
+        bias[:, ROWS:] = hidden
+
+    def exact(tile, base):
         keys, values = operands(tile)
-        set_bias(base, order)
+        set_bias(base)
 
         for p in range(HEADS // 2):
             h = 2 * p
@@ -135,10 +132,10 @@
                 stat[at : at + 1] = stat[at : at + 1] * fade[:, cols] + part[WIDTH : WIDTH + 1, cols]
                 stat[h + k : h + k + 1] = new[:, cols]
 
-    def quick(tile, base, order, masked):
+    def quick(tile, base, masked):
         keys, values = operands(tile)
         if masked:
-            set_bias(base, order)
+            set_bias(base)
         for p in range(HEADS // 2):
             h = 2 * p
             held = pair_rows(stat, h)
@@ -170,7 +167,7 @@
         for n, (kv_ref, (slots, place)) in enumerate(zip(kv_refs, places)):
 
             def body(i, _, kv_ref=kv_ref, place=place, own_tile=first and n == 0):
-                load, tile_group, order = place(kv_ref, i, group)
+                load, tile_group = place(kv_ref, i, group)
                 base = tile_group * span
                 needed = (base + span > start_low) & (base < q_first + ROWS) & (base >= 0)
                 whole = (base >= start_high) & (base + span <= q_first)
@@ -178,24 +175,24 @@
 
                     @pl.when(needed)
                     def _():
-                        exact(load(), base, order)
+                        exact(load(), base)
 
                     return 0
 
                 @pl.when(needed & whole)
                 def _():
-                    quick(load(), base, order, False)
+                    quick(load(), base, False)
 
                 @pl.when(needed & jnp.logical_not(whole))
                 def _():
-                    quick(load(), base, order, True)
+                    quick(load(), base, True)
 
                 return 0
 
             start = 0
             if fast and first and n == 0:
-                load, tile_group, order = place(kv_ref, 0, group)
-                exact(load(), tile_group * span, order)
+                load, tile_group = place(kv_ref, 0, group)
+                exact(load(), tile_group * span)
                 start = 1
             lax.fori_loop(start, slots, body, 0)
 
@@ -207,9 +204,10 @@
 
     if last:
         stats = stat[...]
+        inverse = 1.0 / stats[HEADS:]
         for h in range(HEADS):
             rows = slice(h * WIDTH, (h + 1) * WIDTH)
-            out[:, rows] = (acc[rows] / stats[HEADS + h : HEADS + h + 1]).T.astype(BF16)
+            out[:, rows] = (acc[rows] * inverse[h : h + 1]).T.astype(BF16)
         log_out[...] = stats[:HEADS] * F32(math.log(2.0)) + jnp.log(stats[HEADS:])
 
 
@@ -240,10 +238,9 @@
 
 
 AXES = ("group", "peer")
-TURNS = (0, 1, 3, 2)
-
-
-def tiles(of_other, back, turned=False):
+
+
+def tiles(of_other, back):
     def at(kv_ref, i, group):
         def load():
             return kv_ref[:, pl.ds(pl.multiple_of(i * ROWS, ROWS), ROWS), :].reshape(BLOCKS * ROWS, 2 * WIDTH)
@@ -251,10 +248,9 @@
         line, core = group // 2, group % 2
         if of_other:
             core = 1 - core
-        order = TURNS if turned else range(BLOCKS)
         if not back:
-            return load, 2 * line + core, order
-        return load, 2 * (line - back - core) + jnp.where(i == 0, core, 1 - core), order
+            return load, 2 * line + core
+        return load, 2 * (line - back - core) + jnp.where(i == 0, core, 1 - core)
 
     return at
 
@@ -281,25 +277,22 @@
     chip = jnp.concatenate([keys_values, swapped(keys_values)], axis=0)
     pair_near = moved(chip, lambda t: t - 8 - 8 * (t // 4 % 2))
     own_mine = across(spread(keys_values))
+    starts = row_starts(doc_lengths, own)
+    near_mine = across(spread(pair_near))
+    pair_far = moved(pair_near, lambda t: t - 16)
     own_other = swapped(own_mine)
-    pair_far = moved(chip, lambda t: t - 24 - 8 * (t // 4 % 2))
-    starts = row_starts(doc_lengths, own)
     prepared = query_pairs(queries), starts
 
     def step(pieces, state, last=False):
         return attend(doc_lengths, prepared, pieces, state, last, own)
 
     state = step([(own_mine, tiles(False, 0)), (own_other, tiles(True, 0))], None)
-    near_mine = across(spread(pair_near))
-    turns = []
-    for k in (1, 3, 2):
-        turns.append(moved(pair_far, lambda t, k=k: t // 4 * 4 + (t + k) % 4))
-    far_mine = jnp.concatenate([pair_far, *turns], axis=0).reshape(BLOCKS, *pair_far.shape)
     near_other = swapped(near_mine)
-    state = step([(near_mine, tiles(False, 1))], state)
+    far_mine = across(spread(pair_far))
+    state = step([(near_mine, tiles(False, 1)), (near_other, tiles(True, 1))], state)
     far_other = swapped(far_mine)
-    state = step([(near_other, tiles(True, 1)), (far_mine, tiles(False, 3, True))], state)
-    attended, log_total = step([(far_other, tiles(True, 3, True))], state, True)
+    state = step([(far_mine, tiles(False, 3))], state)
+    attended, log_total = step([(far_other, tiles(True, 3))], state, True)
     return attended, log_total.T
 
 

time: 97.1 us -> 94.1 us (0.969)
  Pallas kernels: 21.3 us -> 23.9 us
  starting transfers between devices: 41.2 us -> 38.9 us
  blocking collectives: 10.6 us -> 8.97 us
  waiting for transfers between devices: 21.7 us -> 20.1 us
    ppermute x9 -> x6, starting transfers between devices: 37.2 us -> 30.6 us  [moved(): return lax.ppermute(value, AXES, pairs)]
    all_to_all x1 -> x2, starting transfers between devices: 4.01 us -> 8.38 us  [across(): return lax.all_to_all(value, 'peer', 0, 0)]
    pallas_call x4, Pallas kernels: 19.8 us -> 21.5 us  [attend(): pl.pallas_call(functools.partial(attend_body, state is None, last, places...]
    all_to_all x1, blocking collectives: 10.6 us -> 8.97 us  [across(): return lax.all_to_all(value, 'peer', 0, 0)]
    ppermute x9 -> x6, waiting for transfers between devices: 21.7 us -> 20.1 us  [moved(): return lax.ppermute(value, AXES, pairs)]
  transfers between devices with their start and end apart: 10 -> 8, of which waited for: 4 -> 4; matrix products, arithmetic and copies ran while one was open for 1% -> 0% of each run, Pallas kernels for 17% -> 21%
where the time goes in v4:
time: 94.1 us; the launch traced here: 93.6 us
  starting transfers between devices  38.9 us (41%)
  Pallas kernels  23.9 us (25%)
  waiting for transfers between devices  20.1 us (21%)
  blocking collectives  8.97 us (10%)
    ppermute x6, starting transfers between devices, moved(): return lax.ppermute(value, AXES, pairs)  30.6 us
    pallas_call x4, Pallas kernels, attend(): pl.pallas_call(functools.partial(attend_body, state is None, last, places...  21.5 us
    ppermute x6, waiting for transfers between devices, moved(): return lax.ppermute(value, AXES, pairs)  20.1 us
    all_to_all x1, blocking collectives, across(): return lax.all_to_all(value, 'peer', 0, 0)  8.97 us
    all_to_all x2, starting transfers between devices, across(): return lax.all_to_all(value, 'peer', 0, 0)  8.38 us
  transfers between devices with their start and end apart: 8, of which 4 were waited for; matrix products, arithmetic and copies ran while one was open for 0% of the time, Pallas kernels for 21%

profile of v4, /device:TPU:49, one launch (start us, length us, event | category | flops | bytes accessed | tf_op | source)
XLA Modules:
  0.0 93.6 jit_solution(17858673516595776611)
XLA Ops:
  0.6 2.6 %collective-permute-start = (bf16[128,256]{1,0:T(8,128)(2,1)}, bf16[128,256]{1,0:T(8,128)(2,1)S(1)}, u32[]{:S(2)}, u32[]{:S(2)}) collective-permute-start(bf16[128,256]{1,0:T(8,128)(2,1)} %refs_0_.1), channel_id=1, source_target_pairs={{4,0},{5,1},{6,2},{7,3},{0,4},{1,5},{2,6},{3,7},{12,8},{13,9},{14,... | collective-permute-start | bytes 196616 | tf_op jit(solution)/shard_map/ppermute | solution.py:265
  3.2 1.1 %collective-permute-done = bf16[128,256]{1,0:T(8,128)(2,1)S(1)} collective-permute-done((bf16[128,256]{1,0:T(8,128)(2,1)}, bf16[128,256]{1,0:T(8,128)(2,1)S(1)}, u32[]{:S(2)}, u32[]{:S(2)}) %collective-permute-start) | collective-permute-done | bytes 65568 | tf_op jit(solution)/shard_map/ppermute | solution.py:265
  4.3 0.8 pad_maximum_fusion
  5.2 5.8 %collective-permute-start.1 = (bf16[256,256]{1,0:T(8,128)(2,1)S(1)}, bf16[256,256]{1,0:T(8,128)(2,1)S(1)}, u32[]{:S(2)}, u32[]{:S(2)}) collective-permute-start(bf16[256,256]{1,0:T(8,128)(2,1)S(1)} %pad_maximum_fusion), channel_id=1, source_target_pairs={{0,8},{1,9},{2,10},{3,11},{8,16},{9,17},{10,18},{11,19},{4,20},{5,... | collective-permute-start | bytes 393224 | tf_op jit(solution)/shard_map/ppermute | solution.py:265
  11.0 11.7 %collective-permute-done.1.refs_0_ = bf16[256,256]{1,0:T(8,128)(2,1)S(1)} collective-permute-done((bf16[256,256]{1,0:T(8,128)(2,1)S(1)}, bf16[256,256]{1,0:T(8,128)(2,1)S(1)}, u32[]{:S(2)}, u32[]{:S(2)}) %collective-permute-start.1) | collective-permute-done | bytes 131104 | tf_op jit(solution)/shard_map/ppermute | solution.py:265
  22.7 0.8 shard_map.53
  23.5 4.0 %all-to-all-start.1 = ((bf16[4,256,256]{2,1,0:T(8,128)(2,1)}), bf16[4,256,256]{2,1,0:T(8,128)(2,1)S(1)}, u32[]{:S(2)}, u32[]{:S(2)}) async-start(bf16[4,256,256]{2,1,0:T(8,128)(2,1)} %shard_map.53), calls=%async_computation.1 | async-start | bytes 1048576 | tf_op jit(solution)/shard_map/all_to_all | solution.py:269
  27.5 1.9 %collective-permute-start.2 = (bf16[256,256]{1,0:T(8,128)(2,1)S(1)}, bf16[256,256]{1,0:T(8,128)(2,1)S(1)}, u32[]{:S(2)}, u32[]{:S(2)}) collective-permute-start(bf16[256,256]{1,0:T(8,128)(2,1)S(1)} %collective-permute-done.1.refs_0_), channel_id=1, source_target_pairs={{0,16},{1,17},{2,18},{3,19},{4,20},{5,21},{6,22},{7,23},{8,24},{9,... | collective-permute-start | bytes 393224 | tf_op jit(solution)/shard_map/ppermute | solution.py:265
  29.5 6.9 %collective-permute-done.2.refs_0_ = bf16[256,256]{1,0:T(8,128)(2,1)S(1)} collective-permute-done((bf16[256,256]{1,0:T(8,128)(2,1)S(1)}, bf16[256,256]{1,0:T(8,128)(2,1)S(1)}, u32[]{:S(2)}, u32[]{:S(2)}) %collective-permute-start.2) | collective-permute-done | bytes 131104 | tf_op jit(solution)/shard_map/ppermute | solution.py:265
  36.4 0.8 shard_map.52
  37.2 0.0 copy-start.1
  37.2 0.0 all-to-all-done.1.refs_0_
  37.2 4.4 %all-to-all-start = ((bf16[4,256,256]{2,1,0:T(8,128)(2,1)}), bf16[4,256,256]{2,1,0:T(8,128)(2,1)S(1)}, u32[]{:S(2)}, u32[]{:S(2)}) async-start(bf16[4,256,256]{2,1,0:T(8,128)(2,1)} %shard_map.52), calls=%async_computation | async-start | bytes 1048576 | tf_op jit(solution)/shard_map/all_to_all | solution.py:269
  41.6 9.0 %collective-permute-start.4 = (bf16[4,256,256]{2,1,0:T(8,128)(2,1)S(1)}, bf16[4,256,256]{2,1,0:T(8,128)(2,1)S(1)}, u32[]{:S(2)}, u32[]{:S(2)}) collective-permute-start(bf16[4,256,256]{2,1,0:T(8,128)(2,1)S(1)} %all-to-all-done.1.refs_0_), channel_id=1, source_target_pairs={{4,0},{5,1},{6,2},{7,3},{0,4},{1,5},{2,6},{3,7},{12,8},{13,9},{14,... | collective-permute-start | bytes 1572872 | tf_op jit(solution)/shard_map/ppermute | solution.py:265
  50.6 0.0 all-to-all-done.refs_0_
  50.6 8.1 %collective-permute-start.3 = (bf16[4,256,256]{2,1,0:T(8,128)(2,1)S(1)}, bf16[4,256,256]{2,1,0:T(8,128)(2,1)S(1)}, u32[]{:S(2)}, u32[]{:S(2)}) collective-permute-start(bf16[4,256,256]{2,1,0:T(8,128)(2,1)S(1)} %all-to-all-done.refs_0_), channel_id=1, source_target_pairs={{4,0},{5,1},{6,2},{7,3},{0,4},{1,5},{2,6},{3,7},{12,8},{13,9},{14,... | collective-permute-start | bytes 1572872 | tf_op jit(solution)/shard_map/ppermute | solution.py:265
  58.6 0.0 copy-done.1
  58.7 0.0 copy-start
  58.7 9.0 %all_to_all.15.refs_0_ = bf16[4,128,256]{2,1,0:T(8,128)(2,1)S(1)} all-to-all(bf16[4,128,256]{2,1,0:T(8,128)(2,1)S(1)} %shard_map.54), channel_id=1, replica_groups=mesh['group'=192,'peer'=4] {'peer'}, dimensions={0} | all-to-all | bytes 524288 | tf_op jit(solution)/shard_map/all_to_all | solution.py:269
  67.7 0.0 copy-start.2
  67.7 3.2 %collective-permute-start.5 = (bf16[4,128,256]{2,1,0:T(8,128)(2,1)S(1)}, bf16[4,128,256]{2,1,0:T(8,128)(2,1)S(1)}, u32[]{:S(2)}, u32[]{:S(2)}) collective-permute-start(bf16[4,128,256]{2,1,0:T(8,128)(2,1)S(1)} %all_to_all.15.refs_0_), channel_id=1, source_target_pairs={{4,0},{5,1},{6,2},{7,3},{0,4},{1,5},{2,6},{3,7},{12,8},{13,9},{14,... | collective-permute-start | bytes 786440 | tf_op jit(solution)/shard_map/ppermute | solution.py:265
  70.9 0.0 copy-done
  70.9 0.1 shard_map.50.query
  71.0 0.0 copy-done.2
  71.0 0.6 shard_map.51.start_ref
  71.6 0.4 collective-permute-done.5.refs_1_
  72.0 3.5 %shard_map.55 = (f32[16,128]{1,0:T(8,128)S(1)}, f32[1024,128]{1,0:T(8,128)S(1)}) custom-call(s32[25]{0:T(128)S(1)} %copy-done.2, bf16[512,256]{1,0:T(8,128)(2,1)S(1)} %shard_map.50.query, s32[8,128]{1,0:T(8,128)S(1)} %shard_map.51.start_ref, bf16[4,128,256]{2,1,0:T(8,128)(2,1)S(1)} %all_to_all.15.refs_0_, bf16[4,128,256]{2,1,0:T(8,128)(2,1)S(1)} %collective-permute-done.5.refs_1_), custom_call_target="tpu_custom_call" | custom-call | tf_op jit(solution)/shard_map/pallas_call | solution.py:230
  75.5 0.0 collective-permute-done.4.refs_1_
  75.5 12.4 %shard_map.56 = (f32[16,128]{1,0:T(8,128)S(1)}, f32[1024,128]{1,0:T(8,128)S(1)}) custom-call(s32[25]{0:T(128)S(1)} %copy-done.2, bf16[512,256]{1,0:T(8,128)(2,1)S(1)} %shard_map.50.query, s32[8,128]{1,0:T(8,128)S(1)} %shard_map.51.start_ref, bf16[4,256,256]{2,1,0:T(8,128)(2,1)S(1)} %all-to-all-done.1.refs_0_, ...), custom_call_target="tpu_custom_call" | custom-call | tf_op jit(solution)/shard_map/pallas_call | solution.py:230
  87.9 1.9 %shard_map.57 = (f32[16,128]{1,0:T(8,128)S(1)}, f32[1024,128]{1,0:T(8,128)S(1)}) custom-call(s32[25]{0:T(128)S(1)} %copy-done.2, bf16[512,256]{1,0:T(8,128)(2,1)S(1)} %shard_map.50.query, s32[8,128]{1,0:T(8,128)S(1)} %shard_map.51.start_ref, bf16[4,256,256]{2,1,0:T(8,128)(2,1)S(1)} %all-to-all-done.refs_0_, f32[16,128]{1,0:T(8,128)S(1)} %get-tuple-element.12.refs_1_, ...), custom_call_target="tpu_custom_call" | custom-call | tf_op jit(solution)/shard_map/pallas_call | solution.py:230
  89.8 0.0 collective-permute-done.3.refs_0_
  89.8 3.8 %shard_map.58 = (bf16[128,1024]{1,0:T(8,128)(2,1)}, f32[8,128]{1,0:T(8,128)}) custom-call(s32[25]{0:T(128)S(1)} %copy-done.2, bf16[512,256]{1,0:T(8,128)(2,1)S(1)} %shard_map.50.query, s32[8,128]{1,0:T(8,128)S(1)} %shard_map.51.start_ref, bf16[4,256,256]{2,1,0:T(8,128)(2,1)S(1)} %collective-permute-done.3.refs_0_, f32[16,128]{1,0:T(8,128)S(1)} %get-tuple-element.14.refs_1_, ...), custom_call_target="tpu_custom_call" | custom-call | tf_op jit(solution)/shard_map/pallas_call | solution.py:230
  (1 shorter events, 0.0 us)
Async XLA Ops:
  0.6 3.7 %collective-permute-start = (bf16[128,256]{1,0:T(8,128)(2,1)}, bf16[128,256]{1,0:T(8,128)(2,1)S(1)}, u32[]{:S(2)}, u32[]{:S(2)}) collective-permute-start(bf16[128,256]{1,0:T(8,128)(2,1)} %refs_0_.1), channel_id=1, source_target_pairs={{4,0},{5,1},{6,2},{7,3},{0,4},{1,5},{2,6},{3,7},{12,8},{13,9},{14,... | collective-permute-start | bytes 196616 | tf_op jit(solution)/shard_map/ppermute | solution.py:265
  5.2 17.5 %collective-permute-start.1 = (bf16[256,256]{1,0:T(8,128)(2,1)S(1)}, bf16[256,256]{1,0:T(8,128)(2,1)S(1)}, u32[]{:S(2)}, u32[]{:S(2)}) collective-permute-start(bf16[256,256]{1,0:T(8,128)(2,1)S(1)} %pad_maximum_fusion), channel_id=1, source_target_pairs={{0,8},{1,9},{2,10},{3,11},{8,16},{9,17},{10,18},{11,19},{4,20},{5,... | collective-permute-start | bytes 393224 | tf_op jit(solution)/shard_map/ppermute | solution.py:265
  23.5 13.7 %all-to-all-start.1 = ((bf16[4,256,256]{2,1,0:T(8,128)(2,1)}), bf16[4,256,256]{2,1,0:T(8,128)(2,1)S(1)}, u32[]{:S(2)}, u32[]{:S(2)}) async-start(bf16[4,256,256]{2,1,0:T(8,128)(2,1)} %shard_map.53), calls=%async_computation.1 | async-start | bytes 1048576 | tf_op jit(solution)/shard_map/all_to_all | solution.py:269
  27.5 8.8 %collective-permute-start.2 = (bf16[256,256]{1,0:T(8,128)(2,1)S(1)}, bf16[256,256]{1,0:T(8,128)(2,1)S(1)}, u32[]{:S(2)}, u32[]{:S(2)}) collective-permute-start(bf16[256,256]{1,0:T(8,128)(2,1)S(1)} %collective-permute-done.1.refs_0_), channel_id=1, source_target_pairs={{0,16},{1,17},{2,18},{3,19},{4,20},{5,21},{6,22},{7,23},{8,24},{9,... | collective-permute-start | bytes 393224 | tf_op jit(solution)/shard_map/ppermute | solution.py:265
  37.2 21.5 %copy-start.1 = (bf16[128,256]{1,0:T(8,128)(2,1)S(1)}, bf16[128,256]{1,0:T(8,128)(2,1)}, u32[]{:S(2)}) copy-start(bf16[128,256]{1,0:T(8,128)(2,1)} %refs_0_.1) | copy-start | bytes 196612
  37.2 13.4 %all-to-all-start = ((bf16[4,256,256]{2,1,0:T(8,128)(2,1)}), bf16[4,256,256]{2,1,0:T(8,128)(2,1)S(1)}, u32[]{:S(2)}, u32[]{:S(2)}) async-start(bf16[4,256,256]{2,1,0:T(8,128)(2,1)} %shard_map.52), calls=%async_computation | async-start | bytes 1048576 | tf_op jit(solution)/shard_map/all_to_all | solution.py:269
  41.6 33.9 %collective-permute-start.4 = (bf16[4,256,256]{2,1,0:T(8,128)(2,1)S(1)}, bf16[4,256,256]{2,1,0:T(8,128)(2,1)S(1)}, u32[]{:S(2)}, u32[]{:S(2)}) collective-permute-start(bf16[4,256,256]{2,1,0:T(8,128)(2,1)S(1)} %all-to-all-done.1.refs_0_), channel_id=1, source_target_pairs={{4,0},{5,1},{6,2},{7,3},{0,4},{1,5},{2,6},{3,7},{12,8},{13,9},{14,... | collective-permute-start | bytes 1572872 | tf_op jit(solution)/shard_map/ppermute | solution.py:265
  50.6 39.2 %collective-permute-start.3 = (bf16[4,256,256]{2,1,0:T(8,128)(2,1)S(1)}, bf16[4,256,256]{2,1,0:T(8,128)(2,1)S(1)}, u32[]{:S(2)}, u32[]{:S(2)}) collective-permute-start(bf16[4,256,256]{2,1,0:T(8,128)(2,1)S(1)} %all-to-all-done.refs_0_), channel_id=1, source_target_pairs={{4,0},{5,1},{6,2},{7,3},{0,4},{1,5},{2,6},{3,7},{12,8},{13,9},{14,... | collective-permute-start | bytes 1572872 | tf_op jit(solution)/shard_map/ppermute | solution.py:265
  58.7 12.2 %copy-start = (bf16[128,1024]{1,0:T(8,128)(2,1)S(1)}, bf16[128,1024]{1,0:T(8,128)(2,1)}, u32[]{:S(2)}) copy-start(bf16[128,1024]{1,0:T(8,128)(2,1)} %q_ref.1) | copy-start | bytes 786436
  67.7 3.3 %copy-start.2 = (s32[25]{0:T(128)S(1)}, s32[25]{0:T(128)}, u32[]{:S(2)}) copy-start(s32[25]{0:T(128)} %doc_ref.9) | copy-start | bytes 304
  67.7 4.3 %collective-permute-start.5 = (bf16[4,128,256]{2,1,0:T(8,128)(2,1)S(1)}, bf16[4,128,256]{2,1,0:T(8,128)(2,1)S(1)}, u32[]{:S(2)}, u32[]{:S(2)}) collective-permute-start(bf16[4,128,256]{2,1,0:T(8,128)(2,1)S(1)} %all_to_all.15.refs_0_), channel_id=1, source_target_pairs={{4,0},{5,1},{6,2},{7,3},{0,4},{1,5},{2,6},{3,7},{12,8},{13,9},{14,... | collective-permute-start | bytes 786440 | tf_op jit(solution)/shard_map/ppermute | solution.py:265

commit v5 on v2

--- a/solution.py
+++ b/solution.py
@@ -13,6 +13,7 @@
 HEADS = 8
 WIDTH = 128
 BLOCKS = 4
+CHUNK = 256
 NEG = -1e30
 LIMIT = 2.0**40
 SCALE = math.log2(math.e) / math.sqrt(WIDTH)
@@ -138,13 +139,27 @@
         keys, values = operands(tile)
         if masked:
             set_bias(base, order)
-        for p in range(HEADS // 2):
+        steps = [(p, c) for p in range(HEADS // 2) for c in range(0, span, CHUNK)]
+
+        def scores(step):
+            p, c = step
+            return jnp.dot(keys[c : c + CHUNK], query[p * WIDTH : (p + 1) * WIDTH], preferred_element_type=F32)
+
+        ahead = scores(steps[0])
+        part = None
+        for n, (p, c) in enumerate(steps):
             h = 2 * p
-            held = pair_rows(stat, h)
-            score = jnp.dot(keys, query[p * WIDTH : (p + 1) * WIDTH], preferred_element_type=F32) * F32(SCALE) - held
+            score = ahead
+            if n + 1 < len(steps):
+                ahead = scores(steps[n + 1])
+            score = score * F32(SCALE) - pair_rows(stat, h)
             if masked:
-                score = score + bias[...]
-            part = jnp.dot(values, jnp.exp2(score).astype(BF16), preferred_element_type=F32)
+                score = score + bias[c : c + CHUNK]
+            weight = jnp.exp2(score).astype(BF16)
+            piece = jnp.dot(values[:, c : c + CHUNK], weight, preferred_element_type=F32)
+            part = piece if c == 0 else part + piece
+            if c + CHUNK < span:
+                continue
             for k in range(2):
                 rows, cols = slice((h + k) * WIDTH, (h + k + 1) * WIDTH), slice(k * ROWS, (k + 1) * ROWS)
                 acc[rows] += part[:WIDTH, cols]
@@ -156,13 +171,19 @@
             stat[:HEADS] = jnp.full((HEADS, ROWS), NEG, F32)
             stat[HEADS:] = jnp.zeros((HEADS, ROWS), F32)
             acc[...] = jnp.zeros_like(acc)
+            if fast:
+                own_keys = kv_refs[0][peer, :ROWS, :WIDTH].T.astype(F32)
+                for h in range(HEADS):
+                    rows, cols = slice(h // 2 * WIDTH, (h // 2 + 1) * WIDTH), slice(h % 2 * ROWS, (h % 2 + 1) * ROWS)
+                    product = query[rows, cols].astype(F32) * own_keys
+                    stat[h : h + 1] = jnp.sum(product, axis=0, keepdims=True) * F32(SCALE)
         else:
             stat[...] = stat_in[...]
             acc[...] = acc_in[...]
 
-        for n, (kv_ref, (slots, place)) in enumerate(zip(kv_refs, places)):
-
-            def body(i, _, kv_ref=kv_ref, place=place, own_tile=first and n == 0):
+        for kv_ref, (slots, place) in zip(kv_refs, places):
+
+            def body(i, _, kv_ref=kv_ref, place=place):
                 load, tile_group, order = place(kv_ref, i, group)
                 base = tile_group * span
                 needed = (base + span > start_low) & (base < q_first + ROWS) & (base >= 0)
@@ -185,12 +206,7 @@
 
                 return 0
 
-            start = 0
-            if fast and first and n == 0:
-                load, tile_group, order = place(kv_ref, 0, group)
-                exact(load(), tile_group * span, order)
-                start = 1
-            lax.fori_loop(start, slots, body, 0)
+            lax.fori_loop(0, slots, body, 0)
 
     run(True)
 
@@ -200,9 +216,10 @@
 
     if last:
         stats = stat[...]
+        inverse = 1.0 / stats[HEADS:]
         for h in range(HEADS):
             rows = slice(h * WIDTH, (h + 1) * WIDTH)
-            out[:, rows] = (acc[rows] / stats[HEADS + h : HEADS + h + 1]).T.astype(BF16)
+            out[:, rows] = (acc[rows] * inverse[h : h + 1]).T.astype(BF16)
         log_out[...] = stats[:HEADS] * F32(math.log(2.0)) + jnp.log(stats[HEADS:])
 
 
@@ -279,10 +296,8 @@
     far_mine = jnp.concatenate([pair_far, *turns], axis=0).reshape(BLOCKS, *pair_far.shape)
     near_other = moved(near_mine, lambda t: t ^ 4)
     far_other = moved(far_mine, lambda t: t ^ 4)
-    state = attend(doc_lengths, prepared, [(near_mine, tiles(False, near))], None, False, own)
-    state = attend(
-        doc_lengths, prepared, [(near_other, tiles(True, near)), (far_mine, tiles(False, far, True))], state, False, own
-    )
+    pieces = [(near_mine, tiles(False, near)), (near_other, tiles(True, near)), (far_mine, tiles(False, far, True))]
+    state = attend(doc_lengths, prepared, pieces, None, False, own)
     attended, log_total = attend(doc_lengths, prepared, [(far_other, tiles(True, far, True))], state, True, own)
     return attended, log_total.T
 

time: 85.8 us -> 85.9 us (level)
    pallas_call x3 -> x2, Pallas kernels: 22.8 us -> 22.8 us  [attend(): pl.pallas_call(functools.partial(attend_body, state is None, last, places...]
  transfers between devices with their start and end apart: 9 -> 9, of which waited for: 5 -> 5; matrix products, arithmetic and copies ran while one was open for 1% -> 1% of each run, Pallas kernels for 22% -> 24%
where the time goes in v5:
time: 85.9 us; the launch traced here: 85.5 us
  starting transfers between devices  36.3 us (42%)
  Pallas kernels  24.5 us (29%)
  waiting for transfers between devices  23 us (27%)
  local copies, waits for them, and re-layouts  0.87 us (1%)
    ppermute x8, starting transfers between devices, moved(): return lax.ppermute(value, AXES, pairs)  32.3 us
    pallas_call x2, Pallas kernels, attend(): pl.pallas_call(functools.partial(attend_body, state is None, last, places...  22.8 us
    ppermute x8, waiting for transfers between devices, moved(): return lax.ppermute(value, AXES, pairs)  16.6 us
    all_to_all x1, waiting for transfers between devices, shards(): near_mine = lax.all_to_all(spread(keys_values, pair_near), 'peer', 0, 0)  6.36 us
    all_to_all x1, starting transfers between devices, shards(): near_mine = lax.all_to_all(spread(keys_values, pair_near), 'peer', 0, 0)  4.01 us
  transfers between devices with their start and end apart: 9, of which 5 were waited for; matrix products, arithmetic and copies ran while one was open for 1% of the time, Pallas kernels for 24%

profile of v5, /device:TPU:49, one launch (start us, length us, event | category | flops | bytes accessed | tf_op | source)
XLA Modules:
  0.0 85.5 jit_solution(16990944133131082329)
XLA Ops:
  0.6 2.6 %collective-permute-start = (bf16[128,256]{1,0:T(8,128)(2,1)}, bf16[128,256]{1,0:T(8,128)(2,1)S(1)}, u32[]{:S(2)}, u32[]{:S(2)}) collective-permute-start(bf16[128,256]{1,0:T(8,128)(2,1)} %refs_0_.1), channel_id=1, source_target_pairs={{4,0},{5,1},{6,2},{7,3},{0,4},{1,5},{2,6},{3,7},{12,8},{13,9},{14,... | collective-permute-start | bytes 196616 | tf_op jit(solution)/shard_map/ppermute | solution.py:283
  3.2 0.8 constant_dynamic-update-slice_fusion.1
  4.1 0.0 copy-start.1
  4.1 0.2 collective-permute-done
  4.3 5.8 %collective-permute-start.6 = (bf16[256,256]{1,0:T(8,128)(2,1)S(1)}, bf16[256,256]{1,0:T(8,128)(2,1)S(1)}, u32[]{:S(2)}, u32[]{:S(2)}) collective-permute-start(bf16[256,256]{1,0:T(8,128)(2,1)S(1)} %constant_dynamic-update-slice_fusion), channel_id=1, source_target_pairs={{0,8},{1,9},{2,10},{3,11},{8,16},{9,17},{10,18},{11,19},{4,20},{5,... | collective-permute-start | bytes 393224 | tf_op jit(solution)/shard_map/ppermute | solution.py:283
  10.1 11.7 %collective-permute-done.6.refs_1_ = bf16[256,256]{1,0:T(8,128)(2,1)S(1)} collective-permute-done((bf16[256,256]{1,0:T(8,128)(2,1)S(1)}, bf16[256,256]{1,0:T(8,128)(2,1)S(1)}, u32[]{:S(2)}, u32[]{:S(2)}) %collective-permute-start.6) | collective-permute-done | bytes 131104 | tf_op jit(solution)/shard_map/ppermute | solution.py:283
  21.8 0.0 copy-done.1
  21.8 1.0 %shard_map.52 = bf16[4,384,256]{2,1,0:T(8,128)(2,1)} custom-call(bf16[128,256]{1,0:T(8,128)(2,1)S(1)} %copy-done.1, bf16[256,256]{1,0:T(8,128)(2,1)S(1)} %collective-permute-done.6.refs_1_), custom_call_target="tpu_custom_call" | custom-call | tf_op jit(solution)/shard_map/pallas_call | solution.py:78
  22.8 4.0 %all-to-all-start = ((bf16[4,384,256]{2,1,0:T(8,128)(2,1)}), bf16[4,384,256]{2,1,0:T(8,128)(2,1)S(1)}, u32[]{:S(2)}, u32[]{:S(2)}) async-start(bf16[4,384,256]{2,1,0:T(8,128)(2,1)} %shard_map.52), calls=%async_computation | async-start | bytes 1572864 | tf_op jit(solution)/shard_map/all_to_all | solution.py:292
  26.8 0.0 copy-start
  26.8 2.0 %collective-permute-start.1 = (bf16[256,256]{1,0:T(8,128)(2,1)S(1)}, bf16[256,256]{1,0:T(8,128)(2,1)S(1)}, u32[]{:S(2)}, u32[]{:S(2)}) collective-permute-start(bf16[256,256]{1,0:T(8,128)(2,1)S(1)} %constant_dynamic-update-slice_fusion), channel_id=1, source_target_pairs={{0,24},{1,25},{2,26},{3,27},{8,32},{9,33},{10,34},{11,35},{4,36},{... | collective-permute-start | bytes 393224 | tf_op jit(solution)/shard_map/ppermute | solution.py:283
  28.9 6.4 %all-to-all-done.refs_0_ = bf16[4,384,256]{2,1,0:T(8,128)(2,1)S(1)} async-done(((bf16[4,384,256]{2,1,0:T(8,128)(2,1)}), bf16[4,384,256]{2,1,0:T(8,128)(2,1)S(1)}, u32[]{:S(2)}, u32[]{:S(2)}) %all-to-all-start) | async-done | bytes 786464 | tf_op jit(solution)/shard_map/all_to_all | solution.py:292
  35.2 6.7 %collective-permute-start.7 = (bf16[4,384,256]{2,1,0:T(8,128)(2,1)S(1)}, bf16[4,384,256]{2,1,0:T(8,128)(2,1)S(1)}, u32[]{:S(2)}, u32[]{:S(2)}) collective-permute-start(bf16[4,384,256]{2,1,0:T(8,128)(2,1)S(1)} %all-to-all-done.refs_0_), channel_id=1, source_target_pairs={{4,0},{5,1},{6,2},{7,3},{0,4},{1,5},{2,6},{3,7},{12,8},{13,9},{14,... | collective-permute-start | bytes 2359304 | tf_op jit(solution)/shard_map/ppermute | solution.py:283
  42.0 0.0 collective-permute-done.1
  42.0 2.8 %collective-permute-start.2 = (bf16[256,256]{1,0:T(8,128)(2,1)S(1)}, bf16[256,256]{1,0:T(8,128)(2,1)S(1)}, u32[]{:S(2)}, u32[]{:S(2)}) collective-permute-start(bf16[256,256]{1,0:T(8,128)(2,1)S(1)} %collective-permute-done.1), channel_id=1, source_target_pairs={{1,0},{2,1},{3,2},{0,3},{5,4},{6,5},{7,6},{4,7},{9,8},{10,9},{11,1... | collective-permute-start | bytes 393224 | tf_op jit(solution)/shard_map/ppermute | solution.py:283
  44.8 2.5 %collective-permute-start.3 = (bf16[256,256]{1,0:T(8,128)(2,1)S(1)}, bf16[256,256]{1,0:T(8,128)(2,1)S(1)}, u32[]{:S(2)}, u32[]{:S(2)}) collective-permute-start(bf16[256,256]{1,0:T(8,128)(2,1)S(1)} %collective-permute-done.1), channel_id=1, source_target_pairs={{3,0},{0,1},{1,2},{2,3},{7,4},{4,5},{5,6},{6,7},{11,8},{8,9},{9,10... | collective-permute-start | bytes 393224 | tf_op jit(solution)/shard_map/ppermute | solution.py:283
  47.3 2.5 %collective-permute-start.4 = (bf16[256,256]{1,0:T(8,128)(2,1)S(1)}, bf16[256,256]{1,0:T(8,128)(2,1)S(1)}, u32[]{:S(2)}, u32[]{:S(2)}) collective-permute-start(bf16[256,256]{1,0:T(8,128)(2,1)S(1)} %collective-permute-done.1), channel_id=1, source_target_pairs={{2,0},{3,1},{0,2},{1,3},{6,4},{7,5},{4,6},{5,7},{10,8},{11,9},{8,1... | collective-permute-start | bytes 393224 | tf_op jit(solution)/shard_map/ppermute | solution.py:283
  49.8 0.0 collective-permute-done.2
  49.8 1.9 %collective-permute-done.3 = bf16[256,256]{1,0:T(8,128)(2,1)S(1)} collective-permute-done((bf16[256,256]{1,0:T(8,128)(2,1)S(1)}, bf16[256,256]{1,0:T(8,128)(2,1)S(1)}, u32[]{:S(2)}, u32[]{:S(2)}) %collective-permute-start.3) | collective-permute-done | bytes 131104 | tf_op jit(solution)/shard_map/ppermute | solution.py:283
  51.7 2.8 %collective-permute-done.4 = bf16[256,256]{1,0:T(8,128)(2,1)S(1)} collective-permute-done((bf16[256,256]{1,0:T(8,128)(2,1)S(1)}, bf16[256,256]{1,0:T(8,128)(2,1)S(1)}, u32[]{:S(2)}, u32[]{:S(2)}) %collective-permute-start.4) | collective-permute-done | bytes 131104 | tf_op jit(solution)/shard_map/ppermute | solution.py:283
  54.5 0.0 copy-start.2
  54.5 7.3 %collective-permute-start.5 = (bf16[4,256,256]{2,1,0:T(8,128)(2,1)S(1)}, bf16[4,256,256]{2,1,0:T(8,128)(2,1)S(1)}, u32[]{:S(2)}, u32[]{:S(2)}) collective-permute-start(bf16[4,256,256]{2,1,0:T(8,128)(2,1)S(1)} %bitcast.2), channel_id=1, source_target_pairs={{4,0},{5,1},{6,2},{7,3},{0,4},{1,5},{2,6},{3,7},{12,8},{13,9},{14,... | collective-permute-start | bytes 1572872 | tf_op jit(solution)/shard_map/ppermute | solution.py:283
  61.9 0.0 copy-done
  61.9 0.1 shard_map.50.query
  62.0 0.0 copy-done.2
  62.0 0.6 shard_map.51.start_ref
  62.6 0.0 collective-permute-done.7.refs_1_
  62.6 19.4 %shard_map.53 = (f32[16,128]{1,0:T(8,128)S(1)}, f32[1024,128]{1,0:T(8,128)S(1)}) custom-call(s32[25]{0:T(128)S(1)} %copy-done.2, bf16[512,256]{1,0:T(8,128)(2,1)S(1)} %shard_map.50.query, s32[8,128]{1,0:T(8,128)S(1)} %shard_map.51.start_ref, bf16[4,384,256]{2,1,0:T(8,128)(2,1)S(1)} %all-to-all-done.refs_0_, ...), custom_call_target="tpu_custom_call" | custom-call | tf_op jit(solution)/shard_map/pallas_call | solution.py:242
  82.1 0.0 collective-permute-done.5.refs_0_
  82.1 3.4 %shard_map.54 = (bf16[128,1024]{1,0:T(8,128)(2,1)}, f32[8,128]{1,0:T(8,128)}) custom-call(s32[25]{0:T(128)S(1)} %copy-done.2, bf16[512,256]{1,0:T(8,128)(2,1)S(1)} %shard_map.50.query, s32[8,128]{1,0:T(8,128)S(1)} %shard_map.51.start_ref, bf16[4,256,256]{2,1,0:T(8,128)(2,1)S(1)} %collective-permute-done.5.refs_0_, f32[16,128]{1,0:T(8,128)S(1)} %get-tuple-element.6.refs_1_, ...), custom_call_target="tpu_custom_call" | custom-call | tf_op jit(solution)/shard_map/pallas_call | solution.py:242
  (2 shorter events, 0.0 us)
Async XLA Ops:
  0.6 3.7 %collective-permute-start = (bf16[128,256]{1,0:T(8,128)(2,1)}, bf16[128,256]{1,0:T(8,128)(2,1)S(1)}, u32[]{:S(2)}, u32[]{:S(2)}) collective-permute-start(bf16[128,256]{1,0:T(8,128)(2,1)} %refs_0_.1), channel_id=1, source_target_pairs={{4,0},{5,1},{6,2},{7,3},{0,4},{1,5},{2,6},{3,7},{12,8},{13,9},{14,... | collective-permute-start | bytes 196616 | tf_op jit(solution)/shard_map/ppermute | solution.py:283
  4.1 17.8 %copy-start.1 = (bf16[128,256]{1,0:T(8,128)(2,1)S(1)}, bf16[128,256]{1,0:T(8,128)(2,1)}, u32[]{:S(2)}) copy-start(bf16[128,256]{1,0:T(8,128)(2,1)} %refs_0_.1) | copy-start | bytes 196612
  4.3 17.5 %collective-permute-start.6 = (bf16[256,256]{1,0:T(8,128)(2,1)S(1)}, bf16[256,256]{1,0:T(8,128)(2,1)S(1)}, u32[]{:S(2)}, u32[]{:S(2)}) collective-permute-start(bf16[256,256]{1,0:T(8,128)(2,1)S(1)} %constant_dynamic-update-slice_fusion), channel_id=1, source_target_pairs={{0,8},{1,9},{2,10},{3,11},{8,16},{9,17},{10,18},{11,19},{4,20},{5,... | collective-permute-start | bytes 393224 | tf_op jit(solution)/shard_map/ppermute | solution.py:283
  22.8 12.4 %all-to-all-start = ((bf16[4,384,256]{2,1,0:T(8,128)(2,1)}), bf16[4,384,256]{2,1,0:T(8,128)(2,1)S(1)}, u32[]{:S(2)}, u32[]{:S(2)}) async-start(bf16[4,384,256]{2,1,0:T(8,128)(2,1)} %shard_map.52), calls=%async_computation | async-start | bytes 1572864 | tf_op jit(solution)/shard_map/all_to_all | solution.py:292
  26.8 35.1 %copy-start = (bf16[128,1024]{1,0:T(8,128)(2,1)S(1)}, bf16[128,1024]{1,0:T(8,128)(2,1)}, u32[]{:S(2)}) copy-start(bf16[128,1024]{1,0:T(8,128)(2,1)} %q_ref.1) | copy-start | bytes 786436
  26.8 15.1 %collective-permute-start.1 = (bf16[256,256]{1,0:T(8,128)(2,1)S(1)}, bf16[256,256]{1,0:T(8,128)(2,1)S(1)}, u32[]{:S(2)}, u32[]{:S(2)}) collective-permute-start(bf16[256,256]{1,0:T(8,128)(2,1)S(1)} %constant_dynamic-update-slice_fusion), channel_id=1, source_target_pairs={{0,24},{1,25},{2,26},{3,27},{8,32},{9,33},{10,34},{11,35},{4,36},{... | collective-permute-start | bytes 393224 | tf_op jit(solution)/shard_map/ppermute | solution.py:283
  35.2 27.4 %collective-permute-start.7 = (bf16[4,384,256]{2,1,0:T(8,128)(2,1)S(1)}, bf16[4,384,256]{2,1,0:T(8,128)(2,1)S(1)}, u32[]{:S(2)}, u32[]{:S(2)}) collective-permute-start(bf16[4,384,256]{2,1,0:T(8,128)(2,1)S(1)} %all-to-all-done.refs_0_), channel_id=1, source_target_pairs={{4,0},{5,1},{6,2},{7,3},{0,4},{1,5},{2,6},{3,7},{12,8},{13,9},{14,... | collective-permute-start | bytes 2359304 | tf_op jit(solution)/shard_map/ppermute | solution.py:283
  42.0 7.8 %collective-permute-start.2 = (bf16[256,256]{1,0:T(8,128)(2,1)S(1)}, bf16[256,256]{1,0:T(8,128)(2,1)S(1)}, u32[]{:S(2)}, u32[]{:S(2)}) collective-permute-start(bf16[256,256]{1,0:T(8,128)(2,1)S(1)} %collective-permute-done.1), channel_id=1, source_target_pairs={{1,0},{2,1},{3,2},{0,3},{5,4},{6,5},{7,6},{4,7},{9,8},{10,9},{11,1... | collective-permute-start | bytes 393224 | tf_op jit(solution)/shard_map/ppermute | solution.py:283
  44.8 6.9 %collective-permute-start.3 = (bf16[256,256]{1,0:T(8,128)(2,1)S(1)}, bf16[256,256]{1,0:T(8,128)(2,1)S(1)}, u32[]{:S(2)}, u32[]{:S(2)}) collective-permute-start(bf16[256,256]{1,0:T(8,128)(2,1)S(1)} %collective-permute-done.1), channel_id=1, source_target_pairs={{3,0},{0,1},{1,2},{2,3},{7,4},{4,5},{5,6},{6,7},{11,8},{8,9},{9,10... | collective-permute-start | bytes 393224 | tf_op jit(solution)/shard_map/ppermute | solution.py:283
  47.3 7.2 %collective-permute-start.4 = (bf16[256,256]{1,0:T(8,128)(2,1)S(1)}, bf16[256,256]{1,0:T(8,128)(2,1)S(1)}, u32[]{:S(2)}, u32[]{:S(2)}) collective-permute-start(bf16[256,256]{1,0:T(8,128)(2,1)S(1)} %collective-permute-done.1), channel_id=1, source_target_pairs={{2,0},{3,1},{0,2},{1,3},{6,4},{7,5},{4,6},{5,7},{10,8},{11,9},{8,1... | collective-permute-start | bytes 393224 | tf_op jit(solution)/shard_map/ppermute | solution.py:283
  54.5 7.5 %copy-start.2 = (s32[25]{0:T(128)S(1)}, s32[25]{0:T(128)}, u32[]{:S(2)}) copy-start(s32[25]{0:T(128)} %doc_ref.5) | copy-start | bytes 304
  54.5 27.5 %collective-permute-start.5 = (bf16[4,256,256]{2,1,0:T(8,128)(2,1)S(1)}, bf16[4,256,256]{2,1,0:T(8,128)(2,1)S(1)}, u32[]{:S(2)}, u32[]{:S(2)}) collective-permute-start(bf16[4,256,256]{2,1,0:T(8,128)(2,1)S(1)} %bitcast.2), channel_id=1, source_target_pairs={{4,0},{5,1},{6,2},{7,3},{0,4},{1,5},{2,6},{3,7},{12,8},{13,9},{14,... | collective-permute-start | bytes 1572872 | tf_op jit(solution)/shard_map/ppermute | solution.py:283

commit v6 on v5

--- a/solution.py
+++ b/solution.py
@@ -296,8 +296,9 @@
     far_mine = jnp.concatenate([pair_far, *turns], axis=0).reshape(BLOCKS, *pair_far.shape)
     near_other = moved(near_mine, lambda t: t ^ 4)
     far_other = moved(far_mine, lambda t: t ^ 4)
-    pieces = [(near_mine, tiles(False, near)), (near_other, tiles(True, near)), (far_mine, tiles(False, far, True))]
-    state = attend(doc_lengths, prepared, pieces, None, False, own)
+    state = attend(doc_lengths, prepared, [(near_mine, tiles(False, near))], None, False, own)
+    pieces = [(near_other, tiles(True, near)), (far_mine, tiles(False, far, True))]
+    state = attend(doc_lengths, prepared, pieces, state, False, own)
     attended, log_total = attend(doc_lengths, prepared, [(far_other, tiles(True, far, True))], state, True, own)
     return attended, log_total.T
 

time: 85.9 us -> 80.4 us (0.936)
  the two profiles are of different devices: /device:TPU:49 before, /device:TPU:54 now
where the time goes in v6:
time: 80.4 us; the launch traced here: 80 us
  waiting for transfers between devices  33.1 us (41%)
  starting transfers between devices  26 us (32%)
  Pallas kernels  19.2 us (24%)
  local copies, waits for them, and re-layouts  0.87 us (1%)
    ppermute x8, waiting for transfers between devices, moved(): return lax.ppermute(value, AXES, pairs)  27.6 us
    ppermute x8, starting transfers between devices, moved(): return lax.ppermute(value, AXES, pairs)  21.3 us
    pallas_call x3, Pallas kernels, attend(): pl.pallas_call(functools.partial(attend_body, state is None, last, places...  17.6 us
    all_to_all x1, waiting for transfers between devices, shards(): near_mine = lax.all_to_all(spread(keys_values, pair_near), 'peer', 0, 0)  5.45 us
    all_to_all x1, starting transfers between devices, shards(): near_mine = lax.all_to_all(spread(keys_values, pair_near), 'peer', 0, 0)  4.77 us
  transfers between devices with their start and end apart: 9, of which 6 were waited for; matrix products, arithmetic and copies ran while one was open for 1% of the time, Pallas kernels for 20%

profile of v6, /device:TPU:54, one launch (start us, length us, event | category | flops | bytes accessed | tf_op | source)
XLA Modules:
  0.0 80.0 jit_solution(264878547828113658)
XLA Ops:
  0.6 1.9 %collective-permute-start = (bf16[128,256]{1,0:T(8,128)(2,1)}, bf16[128,256]{1,0:T(8,128)(2,1)S(1)}, u32[]{:S(2)}, u32[]{:S(2)}) collective-permute-start(bf16[128,256]{1,0:T(8,128)(2,1)} %refs_0_.1), channel_id=1, source_target_pairs={{4,0},{5,1},{6,2},{7,3},{0,4},{1,5},{2,6},{3,7},{12,8},{13,9},{14,... | collective-permute-start | bytes 196616 | tf_op jit(solution)/shard_map/ppermute | solution.py:283
  2.6 0.8 %constant_dynamic-update-slice_fusion.1 = bf16[256,256]{1,0:T(8,128)(2,1)S(1)} fusion(bf16[128,256]{1,0:T(8,128)(2,1)} %refs_0_.1), kind=kLoop, calls=%fused_computation.2 | loop fusion | bytes 131072
  3.4 0.0 copy-start.1
  3.4 0.6 collective-permute-done
  4.0 4.3 %collective-permute-start.6 = (bf16[256,256]{1,0:T(8,128)(2,1)S(1)}, bf16[256,256]{1,0:T(8,128)(2,1)S(1)}, u32[]{:S(2)}, u32[]{:S(2)}) collective-permute-start(bf16[256,256]{1,0:T(8,128)(2,1)S(1)} %constant_dynamic-update-slice_fusion), channel_id=1, source_target_pairs={{0,8},{1,9},{2,10},{3,11},{8,16},{9,17},{10,18},{11,19},{4,20},{5,... | collective-permute-start | bytes 393224 | tf_op jit(solution)/shard_map/ppermute | solution.py:283
  8.3 16.3 %collective-permute-done.6.refs_1_ = bf16[256,256]{1,0:T(8,128)(2,1)S(1)} collective-permute-done((bf16[256,256]{1,0:T(8,128)(2,1)S(1)}, bf16[256,256]{1,0:T(8,128)(2,1)S(1)}, u32[]{:S(2)}, u32[]{:S(2)}) %collective-permute-start.6) | collective-permute-done | bytes 131104 | tf_op jit(solution)/shard_map/ppermute | solution.py:283
  24.6 0.0 copy-done.1
  24.6 1.0 %shard_map.52 = bf16[4,384,256]{2,1,0:T(8,128)(2,1)} custom-call(bf16[128,256]{1,0:T(8,128)(2,1)S(1)} %copy-done.1, bf16[256,256]{1,0:T(8,128)(2,1)S(1)} %collective-permute-done.6.refs_1_), custom_call_target="tpu_custom_call" | custom-call | tf_op jit(solution)/shard_map/pallas_call | solution.py:78
  25.5 4.8 %all-to-all-start = ((bf16[4,384,256]{2,1,0:T(8,128)(2,1)}), bf16[4,384,256]{2,1,0:T(8,128)(2,1)S(1)}, u32[]{:S(2)}, u32[]{:S(2)}) async-start(bf16[4,384,256]{2,1,0:T(8,128)(2,1)} %shard_map.52), calls=%async_computation | async-start | bytes 1572864 | tf_op jit(solution)/shard_map/all_to_all | solution.py:292
  30.3 0.0 copy-start
  30.3 2.0 %collective-permute-start.1 = (bf16[256,256]{1,0:T(8,128)(2,1)S(1)}, bf16[256,256]{1,0:T(8,128)(2,1)S(1)}, u32[]{:S(2)}, u32[]{:S(2)}) collective-permute-start(bf16[256,256]{1,0:T(8,128)(2,1)S(1)} %constant_dynamic-update-slice_fusion), channel_id=1, source_target_pairs={{0,24},{1,25},{2,26},{3,27},{8,32},{9,33},{10,34},{11,35},{4,36},{... | collective-permute-start | bytes 393224 | tf_op jit(solution)/shard_map/ppermute | solution.py:283
  32.3 5.4 %all-to-all-done.refs_0_ = bf16[4,384,256]{2,1,0:T(8,128)(2,1)S(1)} async-done(((bf16[4,384,256]{2,1,0:T(8,128)(2,1)}), bf16[4,384,256]{2,1,0:T(8,128)(2,1)S(1)}, u32[]{:S(2)}, u32[]{:S(2)}) %all-to-all-start) | async-done | bytes 786464 | tf_op jit(solution)/shard_map/all_to_all | solution.py:292
  37.8 1.9 %collective-permute-start.7 = (bf16[4,384,256]{2,1,0:T(8,128)(2,1)S(1)}, bf16[4,384,256]{2,1,0:T(8,128)(2,1)S(1)}, u32[]{:S(2)}, u32[]{:S(2)}) collective-permute-start(bf16[4,384,256]{2,1,0:T(8,128)(2,1)S(1)} %all-to-all-done.refs_0_), channel_id=1, source_target_pairs={{4,0},{5,1},{6,2},{7,3},{0,4},{1,5},{2,6},{3,7},{12,8},{13,9},{14,... | collective-permute-start | bytes 2359304 | tf_op jit(solution)/shard_map/ppermute | solution.py:283
  39.7 4.6 %collective-permute-done.1 = bf16[256,256]{1,0:T(8,128)(2,1)S(1)} collective-permute-done((bf16[256,256]{1,0:T(8,128)(2,1)S(1)}, bf16[256,256]{1,0:T(8,128)(2,1)S(1)}, u32[]{:S(2)}, u32[]{:S(2)}) %collective-permute-start.1) | collective-permute-done | bytes 131104 | tf_op jit(solution)/shard_map/ppermute | solution.py:283
  44.3 2.8 %collective-permute-start.2 = (bf16[256,256]{1,0:T(8,128)(2,1)S(1)}, bf16[256,256]{1,0:T(8,128)(2,1)S(1)}, u32[]{:S(2)}, u32[]{:S(2)}) collective-permute-start(bf16[256,256]{1,0:T(8,128)(2,1)S(1)} %collective-permute-done.1), channel_id=1, source_target_pairs={{1,0},{2,1},{3,2},{0,3},{5,4},{6,5},{7,6},{4,7},{9,8},{10,9},{11,1... | collective-permute-start | bytes 393224 | tf_op jit(solution)/shard_map/ppermute | solution.py:283
  47.0 4.3 %collective-permute-start.3 = (bf16[256,256]{1,0:T(8,128)(2,1)S(1)}, bf16[256,256]{1,0:T(8,128)(2,1)S(1)}, u32[]{:S(2)}, u32[]{:S(2)}) collective-permute-start(bf16[256,256]{1,0:T(8,128)(2,1)S(1)} %collective-permute-done.1), channel_id=1, source_target_pairs={{3,0},{0,1},{1,2},{2,3},{7,4},{4,5},{5,6},{6,7},{11,8},{8,9},{9,10... | collective-permute-start | bytes 393224 | tf_op jit(solution)/shard_map/ppermute | solution.py:283
  51.3 2.2 %collective-permute-start.4 = (bf16[256,256]{1,0:T(8,128)(2,1)S(1)}, bf16[256,256]{1,0:T(8,128)(2,1)S(1)}, u32[]{:S(2)}, u32[]{:S(2)}) collective-permute-start(bf16[256,256]{1,0:T(8,128)(2,1)S(1)} %collective-permute-done.1), channel_id=1, source_target_pairs={{2,0},{3,1},{0,2},{1,3},{6,4},{7,5},{4,6},{5,7},{10,8},{11,9},{8,1... | collective-permute-start | bytes 393224 | tf_op jit(solution)/shard_map/ppermute | solution.py:283
  53.5 0.0 collective-permute-done.2
  53.5 0.4 collective-permute-done.3
  53.9 5.8 %collective-permute-done.4 = bf16[256,256]{1,0:T(8,128)(2,1)S(1)} collective-permute-done((bf16[256,256]{1,0:T(8,128)(2,1)S(1)}, bf16[256,256]{1,0:T(8,128)(2,1)S(1)}, u32[]{:S(2)}, u32[]{:S(2)}) %collective-permute-start.4) | collective-permute-done | bytes 131104 | tf_op jit(solution)/shard_map/ppermute | solution.py:283
  59.7 0.0 copy-start.2
  59.8 1.9 %collective-permute-start.5 = (bf16[4,256,256]{2,1,0:T(8,128)(2,1)S(1)}, bf16[4,256,256]{2,1,0:T(8,128)(2,1)S(1)}, u32[]{:S(2)}, u32[]{:S(2)}) collective-permute-start(bf16[4,256,256]{2,1,0:T(8,128)(2,1)S(1)} %bitcast.2), channel_id=1, source_target_pairs={{4,0},{5,1},{6,2},{7,3},{0,4},{1,5},{2,6},{3,7},{12,8},{13,9},{14,... | collective-permute-start | bytes 1572872 | tf_op jit(solution)/shard_map/ppermute | solution.py:283
  61.7 0.0 copy-done
  61.7 0.1 shard_map.50.query
  61.8 0.0 copy-done.2
  61.8 0.6 shard_map.51.start_ref
  62.4 3.6 %shard_map.53 = (f32[16,128]{1,0:T(8,128)S(1)}, f32[1024,128]{1,0:T(8,128)S(1)}) custom-call(s32[25]{0:T(128)S(1)} %copy-done.2, bf16[512,256]{1,0:T(8,128)(2,1)S(1)} %shard_map.50.query, s32[8,128]{1,0:T(8,128)S(1)} %shard_map.51.start_ref, bf16[4,384,256]{2,1,0:T(8,128)(2,1)S(1)} %all-to-all-done.refs_0_), custom_call_target="tpu_custom_call" | custom-call | tf_op jit(solution)/shard_map/pallas_call | solution.py:242
  66.0 0.0 collective-permute-done.7.refs_0_
  66.0 11.4 %shard_map.54 = (f32[16,128]{1,0:T(8,128)S(1)}, f32[1024,128]{1,0:T(8,128)S(1)}) custom-call(s32[25]{0:T(128)S(1)} %copy-done.2, bf16[512,256]{1,0:T(8,128)(2,1)S(1)} %shard_map.50.query, s32[8,128]{1,0:T(8,128)S(1)} %shard_map.51.start_ref, bf16[4,384,256]{2,1,0:T(8,128)(2,1)S(1)} %collective-permute-done.7.refs_0_, bf16[4,256,256]{2,1,0:T(8,128)(2,1)S(1)} %bitcast.3, ...), custom_call_target="tpu_custom_call" | custom-call | tf_op jit(solution)/shard_map/pallas_call | solution.py:242
  77.5 0.0 collective-permute-done.5.refs_0_
  77.5 2.5 %shard_map.55 = (bf16[128,1024]{1,0:T(8,128)(2,1)}, f32[8,128]{1,0:T(8,128)}) custom-call(s32[25]{0:T(128)S(1)} %copy-done.2, bf16[512,256]{1,0:T(8,128)(2,1)S(1)} %shard_map.50.query, s32[8,128]{1,0:T(8,128)S(1)} %shard_map.51.start_ref, bf16[4,256,256]{2,1,0:T(8,128)(2,1)S(1)} %collective-permute-done.5.refs_0_, f32[16,128]{1,0:T(8,128)S(1)} %get-tuple-element.10.refs_1_, ...), custom_call_target="tpu_custom_call" | custom-call | tf_op jit(solution)/shard_map/pallas_call | solution.py:242
  (2 shorter events, 0.0 us)
Async XLA Ops:
  0.6 3.4 %collective-permute-start = (bf16[128,256]{1,0:T(8,128)(2,1)}, bf16[128,256]{1,0:T(8,128)(2,1)S(1)}, u32[]{:S(2)}, u32[]{:S(2)}) collective-permute-start(bf16[128,256]{1,0:T(8,128)(2,1)} %refs_0_.1), channel_id=1, source_target_pairs={{4,0},{5,1},{6,2},{7,3},{0,4},{1,5},{2,6},{3,7},{12,8},{13,9},{14,... | collective-permute-start | bytes 196616 | tf_op jit(solution)/shard_map/ppermute | solution.py:283
  3.4 21.2 %copy-start.1 = (bf16[128,256]{1,0:T(8,128)(2,1)S(1)}, bf16[128,256]{1,0:T(8,128)(2,1)}, u32[]{:S(2)}) copy-start(bf16[128,256]{1,0:T(8,128)(2,1)} %refs_0_.1) | copy-start | bytes 196612
  4.0 20.6 %collective-permute-start.6 = (bf16[256,256]{1,0:T(8,128)(2,1)S(1)}, bf16[256,256]{1,0:T(8,128)(2,1)S(1)}, u32[]{:S(2)}, u32[]{:S(2)}) collective-permute-start(bf16[256,256]{1,0:T(8,128)(2,1)S(1)} %constant_dynamic-update-slice_fusion), channel_id=1, source_target_pairs={{0,8},{1,9},{2,10},{3,11},{8,16},{9,17},{10,18},{11,19},{4,20},{5,... | collective-permute-start | bytes 393224 | tf_op jit(solution)/shard_map/ppermute | solution.py:283
  25.5 12.3 %all-to-all-start = ((bf16[4,384,256]{2,1,0:T(8,128)(2,1)}), bf16[4,384,256]{2,1,0:T(8,128)(2,1)S(1)}, u32[]{:S(2)}, u32[]{:S(2)}) async-start(bf16[4,384,256]{2,1,0:T(8,128)(2,1)} %shard_map.52), calls=%async_computation | async-start | bytes 1572864 | tf_op jit(solution)/shard_map/all_to_all | solution.py:292
  30.3 31.4 %copy-start = (bf16[128,1024]{1,0:T(8,128)(2,1)S(1)}, bf16[128,1024]{1,0:T(8,128)(2,1)}, u32[]{:S(2)}) copy-start(bf16[128,1024]{1,0:T(8,128)(2,1)} %q_ref.1) | copy-start | bytes 786436
  30.3 14.0 %collective-permute-start.1 = (bf16[256,256]{1,0:T(8,128)(2,1)S(1)}, bf16[256,256]{1,0:T(8,128)(2,1)S(1)}, u32[]{:S(2)}, u32[]{:S(2)}) collective-permute-start(bf16[256,256]{1,0:T(8,128)(2,1)S(1)} %constant_dynamic-update-slice_fusion), channel_id=1, source_target_pairs={{0,24},{1,25},{2,26},{3,27},{8,32},{9,33},{10,34},{11,35},{4,36},{... | collective-permute-start | bytes 393224 | tf_op jit(solution)/shard_map/ppermute | solution.py:283
  37.8 28.2 %collective-permute-start.7 = (bf16[4,384,256]{2,1,0:T(8,128)(2,1)S(1)}, bf16[4,384,256]{2,1,0:T(8,128)(2,1)S(1)}, u32[]{:S(2)}, u32[]{:S(2)}) collective-permute-start(bf16[4,384,256]{2,1,0:T(8,128)(2,1)S(1)} %all-to-all-done.refs_0_), channel_id=1, source_target_pairs={{4,0},{5,1},{6,2},{7,3},{0,4},{1,5},{2,6},{3,7},{12,8},{13,9},{14,... | collective-permute-start | bytes 2359304 | tf_op jit(solution)/shard_map/ppermute | solution.py:283
  44.3 9.2 %collective-permute-start.2 = (bf16[256,256]{1,0:T(8,128)(2,1)S(1)}, bf16[256,256]{1,0:T(8,128)(2,1)S(1)}, u32[]{:S(2)}, u32[]{:S(2)}) collective-permute-start(bf16[256,256]{1,0:T(8,128)(2,1)S(1)} %collective-permute-done.1), channel_id=1, source_target_pairs={{1,0},{2,1},{3,2},{0,3},{5,4},{6,5},{7,6},{4,7},{9,8},{10,9},{11,1... | collective-permute-start | bytes 393224 | tf_op jit(solution)/shard_map/ppermute | solution.py:283
  47.0 6.9 %collective-permute-start.3 = (bf16[256,256]{1,0:T(8,128)(2,1)S(1)}, bf16[256,256]{1,0:T(8,128)(2,1)S(1)}, u32[]{:S(2)}, u32[]{:S(2)}) collective-permute-start(bf16[256,256]{1,0:T(8,128)(2,1)S(1)} %collective-permute-done.1), channel_id=1, source_target_pairs={{3,0},{0,1},{1,2},{2,3},{7,4},{4,5},{5,6},{6,7},{11,8},{8,9},{9,10... | collective-permute-start | bytes 393224 | tf_op jit(solution)/shard_map/ppermute | solution.py:283
  51.3 8.4 %collective-permute-start.4 = (bf16[256,256]{1,0:T(8,128)(2,1)S(1)}, bf16[256,256]{1,0:T(8,128)(2,1)S(1)}, u32[]{:S(2)}, u32[]{:S(2)}) collective-permute-start(bf16[256,256]{1,0:T(8,128)(2,1)S(1)} %collective-permute-done.1), channel_id=1, source_target_pairs={{2,0},{3,1},{0,2},{1,3},{6,4},{7,5},{4,6},{5,7},{10,8},{11,9},{8,1... | collective-permute-start | bytes 393224 | tf_op jit(solution)/shard_map/ppermute | solution.py:283
  59.7 2.1 %copy-start.2 = (s32[25]{0:T(128)S(1)}, s32[25]{0:T(128)}, u32[]{:S(2)}) copy-start(s32[25]{0:T(128)} %doc_ref.7) | copy-start | bytes 304
  59.8 17.7 %collective-permute-start.5 = (bf16[4,256,256]{2,1,0:T(8,128)(2,1)S(1)}, bf16[4,256,256]{2,1,0:T(8,128)(2,1)S(1)}, u32[]{:S(2)}, u32[]{:S(2)}) collective-permute-start(bf16[4,256,256]{2,1,0:T(8,128)(2,1)S(1)} %bitcast.2), channel_id=1, source_target_pairs={{4,0},{5,1},{6,2},{7,3},{0,4},{1,5},{2,6},{3,7},{12,8},{13,9},{14,... | collective-permute-start | bytes 1572872 | tf_op jit(solution)/shard_map/ppermute | solution.py:283
